TPU v7x, 256 devices: a whole 4x4x8 slice. The times are simulated.
256 devices in a mesh: tm: 64 (over x, z, core), dp: 4 (over y).
Axes of the slice: x: 4, y: 4, z: 8, core: 2. Of those that a mesh axis runs over, the one named last changes fastest.
Arguments:
- inputs: bfloat16 [4, 32768, 256], P('dp', 'tm'), may hold values from -6 to 6
- grad_stream_out: bfloat16 [4, 32768, 256], P('dp', 'tm'), may hold values from -6 to 6
- grad_skip_out: bfloat16 [4, 32768, 256], P('dp', 'tm'), may hold values from -6 to 6
- sample_weight: float32 [4, 32768], P('dp', 'tm'), may hold values from 0.5 to 6, as said below
- conv_weight: bfloat16 [6, 512, 512], replicated, may hold values from -0.25 to 0.25
- out_weight: bfloat16 [6, 256, 512], replicated, may hold values from -0.375 to 0.375
Outputs:
- grad_inputs: float32 [4, 32768, 256], P('dp', 'tm')
- grad_conv: float32 [6, 512, 512], P(None, 'tm', 'dp')
- grad_out: float32 [6, 256, 512], P(None, 'tm', 'dp')
Inputs may be any that keep to these rules, and one draw needn't show every extreme that they name: `sample_weight`: positive loss weights of each sample.
All inputs are finite; a program needn't handle non-finite values.
Results may differ from a plain program's by a relative error of at most 0.02.
Values may be sent and summed in bfloat16 or wider, within the bound.
A program may use at most 128 MiB of HBM per device.

v0:
```python
import jax
import jax.numpy as jnp
from jax import lax
from jax.sharding import PartitionSpec as P


def shifted(x, axis, by):
    count = lax.axis_size(axis)
    pairs = [(i, i + by) for i in range(count) if 0 <= i + by < count]
    return lax.ppermute(x, axis, pairs)


def project(operand, matrix):
    return jnp.einsum("btc,cd->btd", operand, matrix, preferred_element_type=jnp.float32)


def project_back(operand, matrix):
    return jnp.einsum("btd,cd->btc", operand, matrix, preferred_element_type=jnp.float32)


def outer_sum(left_op, right_op):
    return jnp.einsum("btc,btd->cd", left_op, right_op, preferred_element_type=jnp.float32)


def gated_layer(present, earlier, conv_layer, out_layer, channels):
    preact = project(present, conv_layer[:channels]) + project(earlier, conv_layer[channels:])
    gated = (jnp.tanh(preact[..., :channels]) * jax.nn.sigmoid(preact[..., channels:])).astype(
        jnp.bfloat16
    )
    projected = project(gated, out_layer)
    return (preact, gated, projected)


def body(inputs, grad_stream_out, grad_skip_out, sample_weight, conv_weight, out_weight):
    channels = inputs.shape[2]
    length = inputs.shape[1]
    layers = conv_weight.shape[0]
    weight_sum = lax.psum(jnp.sum(sample_weight), ("tm", "dp"))
    samples_all = sample_weight.size * lax.axis_size("tm") * lax.axis_size("dp")
    weighting = sample_weight * (samples_all / weight_sum)
    stored = []
    stream = inputs.astype(jnp.float32)
    for layer_index in range(layers):
        dilation = 2**layer_index
        present = stream.astype(jnp.bfloat16)
        border = shifted(present[:, length - dilation :], "tm", 1)
        earlier = jnp.concatenate([border, present[:, : length - dilation]], axis=1)
        preact, gated, projected = gated_layer(
            present, earlier, conv_weight[layer_index], out_weight[layer_index], channels
        )
        stream = stream + projected[..., :channels]
        stored.append((present, earlier, preact, gated))
    grad_stream = grad_stream_out.astype(jnp.float32) * weighting[..., None]
    grad_skips = grad_skip_out.astype(jnp.float32) * weighting[..., None]
    conv_grads = [None] * layers
    out_grads = [None] * layers
    for layer_index in reversed(range(layers)):
        dilation = 2**layer_index
        present, earlier, preact, gated = stored[layer_index]
        grad_proj = jnp.concatenate([grad_stream, grad_skips], axis=-1).astype(jnp.bfloat16)
        out_grads[layer_index] = outer_sum(gated, grad_proj)
        grad_gated = project_back(grad_proj, out_weight[layer_index])
        filtered = jnp.tanh(preact[..., :channels])
        opening = jax.nn.sigmoid(preact[..., channels:])
        grad_preact = jnp.concatenate(
            [
                grad_gated * opening * (1.0 - filtered * filtered),
                grad_gated * filtered * opening * (1.0 - opening),
            ],
            axis=-1,
        ).astype(jnp.bfloat16)
        conv_grads[layer_index] = jnp.concatenate(
            [outer_sum(present, grad_preact), outer_sum(earlier, grad_preact)], axis=0
        )
        incoming = shifted(grad_preact[:, :dilation], "tm", -1)
        later_rows = jnp.concatenate([grad_preact[:, dilation:], incoming], axis=1)
        grad_stream = (
            grad_stream
            + project_back(grad_preact, conv_weight[layer_index, :channels])
            + project_back(later_rows, conv_weight[layer_index, channels:])
        )
    conv_all = jnp.stack(conv_grads)
    out_all = jnp.stack(out_grads)
    partial_grads = (
        lax.psum_scatter(
            conv_all.astype(jnp.bfloat16), "dp", scatter_dimension=2, tiled=True
        ).astype(jnp.float32),
        lax.psum_scatter(
            out_all.astype(jnp.bfloat16), "dp", scatter_dimension=2, tiled=True
        ).astype(jnp.float32),
    )
    summed = (
        lax.psum_scatter(partial_grads[0], "tm", scatter_dimension=1, tiled=True),
        lax.psum_scatter(partial_grads[1], "tm", scatter_dimension=1, tiled=True),
    )
    return (grad_stream, summed[0], summed[1])


def solution(mesh):
    placed = (
        P("dp", "tm", None),
        P("dp", "tm", None),
        P("dp", "tm", None),
        P("dp", "tm"),
        P(),
        P(),
    )
    return jax.shard_map(
        body,
        mesh=mesh,
        in_specs=placed,
        out_specs=(P("dp", "tm", None), P(None, "tm", "dp"), P(None, "tm", "dp")),
        check_vma=False,
    )
```

profile of v0, /device:TPU:1, one launch (start us, length us, event | category | flops | bytes accessed | tf_op | source)
XLA Modules:
  0.0 539.1 jit_solution(5502163667945407909)
XLA Ops:
  9.5 4.9 collective-permute-start
  14.4 79.7 %psum.7 = f32[]{:T(128)} all-reduce(f32[]{:T(128)} %reduce_sum.9), channel_id=1, replica_groups=mesh['tm'=64,'dp'=4] {'tm','dp'}, use_global_device_ids=true, to_apply=%region_1.0 | all-reduce | flops 1 | bytes 8 | tf_op jit(solution)/shard_map/psum | solution.py:38
  102.8 3.3 collective-permute-start.1
  107.9 4.2 collective-permute-start.2
  113.8 4.2 collective-permute-start.3
  119.9 4.2 collective-permute-start.4
  126.7 4.2 collective-permute-start.5
  136.1 4.6 collective-permute-done.6
  145.2 3.8 collective-permute-done.7
  153.2 4.0 collective-permute-done.8
  161.4 4.0 collective-permute-done.9
  169.5 4.0 collective-permute-done.10
  181.0 7.8 %copy.21 = bf16[6,512,512]{1,0,2:T(8,128)(2,1)} copy(bf16[6,512,512]{2,1,0:T(8,128)(2,1)} %fusion.67) | data formatting | bytes 6291456
  188.7 5.5 %copy.27 = bf16[64,8,6,512]{3,1,2,0:T(8,128)(2,1)} copy(bf16[64,8,6,512]{3,2,1,0:T(8,128)(2,1)} %bitcast.368) | data formatting | bytes 6291456
  197.4 2.3 fusion.22
  205.0 4.4 copy.23
  209.4 3.2 copy.28
  212.9 35.8 %reduce-scatter.11.cloned.1.call-done = bf16[128,3072]{1,0:T(8,128)(2,1)} async-done(((bf16[512,3072]{1,0:T(8,128)(2,1)}), bf16[128,3072]{1,0:T(8,128)(2,1)}) %reduce-scatter.11.cloned.1.call-update) | async-done | bytes 786448
  248.7 2.8 reshape.519
  251.4 2.5 copy.22
  253.9 2.4 convert_element_type.166
  258.5 2.5 collective-permute-start.11
  268.4 9.8 %reduce-scatter.13.cloned.1.call-done = bf16[128,1536]{1,0:T(8,128)(2,1)} async-done(((bf16[512,1536]{1,0:T(8,128)(2,1)}), bf16[128,1536]{1,0:T(8,128)(2,1)}) %reduce-scatter.13.cloned.1.call-update) | async-done | bytes 393232
  280.1 251.9 %all-reduce.2 = f32[6,256,128]{2,1,0:T(8,128)S(1)} all-reduce(bf16[6,256,128]{2,1,0:T(8,128)(2,1)S(1)} %copy.24), channel_id=5, replica_groups=mesh['tm'=64,'dp'=4] {'tm'}, use_global_device_ids=true, to_apply=%region_5.0.clone | all-reduce | flops 196608 | bytes 1179648
  (183 shorter events, 67.1 us)
Async XLA Ops:
  7.2 94.6 %copy-start.2 = (bf16[1,512,256]{2,1,0:T(8,128)(2,1)S(1)}, bf16[1,512,256]{2,1,0:T(8,128)(2,1)}, u32[]{:S(2)}) copy-start(bf16[1,512,256]{2,1,0:T(8,128)(2,1)} %param.6) | copy-start | bytes 786436
  7.2 94.6 %copy-start = (bf16[6,512,512]{2,1,0:T(8,128)(2,1)S(1)}, bf16[6,512,512]{2,1,0:T(8,128)(2,1)}, u32[]{:S(2)}) copy-start(bf16[6,512,512]{2,1,0:T(8,128)(2,1)} %param.10) | copy-start | bytes 9437188
  7.2 241.5 %reduce-scatter.11.cloned.1.call-start = ((), (), s32[]{:S(2)}) async-start(), calls=%async_computation.4 | async-start | bytes 3932160
  9.5 92.2 %collective-permute-start = (bf16[1,1,256]{2,1,0:T(2,128)(2,1)S(1)}, bf16[1,1,256]{2,1,0:T(2,128)(2,1)S(1)}, u32[]{:S(2)}, u32[]{:S(2)}) collective-permute-start(bf16[1,1,256]{2,1,0:T(2,128)(2,1)S(1)} %slice.263), channel_id=1, source_target_pairs={{0,4},{4,8},{8,12},{12,16},{16,20},{20,24},{24,28},{28,32},{32,36}... | collective-permute-start | bytes 1544 | tf_op jit(solution)/shard_map/ppermute | solution.py:10
  101.7 30.4 %copy-start.25 = (bf16[512,256]{0,1:T(8,128)(2,1)}, bf16[512,256]{0,1:T(8,128)(2,1)S(1)}, u32[]{:S(2)}) copy-start(bf16[512,256]{0,1:T(8,128)(2,1)S(1)} %get-tuple-element.23) | copy-start | bytes 786436
  101.7 73.0 %copy-start.27 = (bf16[512,256]{0,1:T(8,128)(2,1)}, bf16[512,256]{0,1:T(8,128)(2,1)S(1)}, u32[]{:S(2)}) copy-start(bf16[512,256]{0,1:T(8,128)(2,1)S(1)} %get-tuple-element.24) | copy-start | bytes 786436
  102.8 4.0 collective-permute-start.1
  107.9 4.9 collective-permute-start.2
  113.8 4.9 collective-permute-start.3
  119.9 5.0 collective-permute-start.4
  126.7 5.0 collective-permute-start.5
  133.9 6.8 %collective-permute-start.6 = (bf16[1,32,512]{1,2,0:T(8,128)(2,1)S(1)}, bf16[1,32,512]{1,2,0:T(8,128)(2,1)S(1)}, u32[]{:S(2)}, u32[]{:S(2)}) collective-permute-start(bf16[1,32,512]{1,2,0:T(8,128)(2,1)S(1)} %pad_maximum_fusion.47), channel_id=1, source_target_pairs={{4,0},{8,4},{12,8},{16,12},{20,16},{24,20},{28,24},{32,28},{36,32}... | collective-permute-start | bytes 98312 | tf_op jit(solution)/shard_map/ppermute | solution.py:10
  142.8 6.3 %collective-permute-start.7 = (bf16[1,16,512]{1,2,0:T(8,128)(2,1)S(1)}, bf16[1,16,512]{1,2,0:T(8,128)(2,1)S(1)}, u32[]{:S(2)}, u32[]{:S(2)}) collective-permute-start(bf16[1,16,512]{1,2,0:T(8,128)(2,1)S(1)} %pad_maximum_fusion.46), channel_id=1, source_target_pairs={{4,0},{8,4},{12,8},{16,12},{20,16},{24,20},{28,24},{32,28},{36,32}... | collective-permute-start | bytes 49160 | tf_op jit(solution)/shard_map/ppermute | solution.py:10
  150.9 6.3 %collective-permute-start.8 = (bf16[1,8,512]{1,2,0:T(8,128)(2,1)S(1)}, bf16[1,8,512]{1,2,0:T(8,128)(2,1)S(1)}, u32[]{:S(2)}, u32[]{:S(2)}) collective-permute-start(bf16[1,8,512]{1,2,0:T(8,128)(2,1)S(1)} %pad_maximum_fusion.45), channel_id=1, source_target_pairs={{4,0},{8,4},{12,8},{16,12},{20,16},{24,20},{28,24},{32,28},{36,32}... | collective-permute-start | bytes 24584 | tf_op jit(solution)/shard_map/ppermute | solution.py:10
  159.1 6.3 %collective-permute-start.9 = (bf16[1,4,512]{1,2,0:T(8,128)(2,1)S(1)}, bf16[1,4,512]{1,2,0:T(8,128)(2,1)S(1)}, u32[]{:S(2)}, u32[]{:S(2)}) collective-permute-start(bf16[1,4,512]{1,2,0:T(8,128)(2,1)S(1)} %pad_maximum_fusion.44), channel_id=1, source_target_pairs={{4,0},{8,4},{12,8},{16,12},{20,16},{24,20},{28,24},{32,28},{36,32}... | collective-permute-start | bytes 12296 | tf_op jit(solution)/shard_map/ppermute | solution.py:10
  167.2 6.3 %collective-permute-start.10 = (bf16[1,2,512]{1,2,0:T(8,128)(2,1)S(1)}, bf16[1,2,512]{1,2,0:T(8,128)(2,1)S(1)}, u32[]{:S(2)}, u32[]{:S(2)}) collective-permute-start(bf16[1,2,512]{1,2,0:T(8,128)(2,1)S(1)} %pad_maximum_fusion.43), channel_id=1, source_target_pairs={{4,0},{8,4},{12,8},{16,12},{20,16},{24,20},{28,24},{32,28},{36,32}... | collective-permute-start | bytes 6152 | tf_op jit(solution)/shard_map/ppermute | solution.py:10
  194.3 84.0 %reduce-scatter.13.cloned.1.call-start = ((), (), s32[]{:S(2)}) async-start(), calls=%async_computation.5 | async-start | bytes 1966080
  195.2 6.6 %copy-start.14 = (bf16[512,256]{0,1:T(8,128)(2,1)S(1)}, bf16[512,256]{0,1:T(8,128)(2,1)}, u32[]{:S(2)}) copy-start(bf16[512,256]{0,1:T(8,128)(2,1)} %copy-done.13) | copy-start | bytes 786436
  195.2 6.6 %copy-start.21 = (bf16[512,256]{0,1:T(8,128)(2,1)S(1)}, bf16[512,256]{0,1:T(8,128)(2,1)}, u32[]{:S(2)}) copy-start(bf16[512,256]{0,1:T(8,128)(2,1)} %copy-done.20) | copy-start | bytes 786436
  195.2 6.6 %copy-start.28 = (bf16[512,256]{0,1:T(8,128)(2,1)S(1)}, bf16[512,256]{0,1:T(8,128)(2,1)}, u32[]{:S(2)}) copy-start(bf16[512,256]{0,1:T(8,128)(2,1)} %copy-done.27) | copy-start | bytes 786436
  195.2 7.6 %copy-start.16 = (bf16[512,256]{0,1:T(8,128)(2,1)S(1)}, bf16[512,256]{0,1:T(8,128)(2,1)}, u32[]{:S(2)}) copy-start(bf16[512,256]{0,1:T(8,128)(2,1)} %copy-done.15) | copy-start | bytes 786436
  195.2 7.6 %copy-start.19 = (bf16[512,256]{0,1:T(8,128)(2,1)S(1)}, bf16[512,256]{0,1:T(8,128)(2,1)}, u32[]{:S(2)}) copy-start(bf16[512,256]{0,1:T(8,128)(2,1)} %copy-done.18) | copy-start | bytes 786436
  212.6 320.0 %reduce-scatter.9.cloned.1.call-start = ((), (), s32[]{:S(2)}) async-start(), calls=%async_computation.3 | async-start | bytes 1597440 | tf_op jit(solution)/shard_map/reduce_scatter | solution.py:93
  258.5 6.7 %collective-permute-start.11 = (bf16[1,1,512]{1,2,0:T(8,128)(2,1)S(1)}, bf16[1,1,512]{1,2,0:T(8,128)(2,1)S(1)}, u32[]{:S(2)}, u32[]{:S(2)}) collective-permute-start(bf16[1,1,512]{1,2,0:T(8,128)(2,1)S(1)} %pad_maximum_fusion.42), channel_id=1, source_target_pairs={{4,0},{8,4},{12,8},{16,12},{20,16},{24,20},{28,24},{32,28},{36,32}... | collective-permute-start | bytes 3080 | tf_op jit(solution)/shard_map/ppermute | solution.py:10
  (21 other events, 65.5 us)
Sparse Core Ops, SparseCore 0:
  194.4 54.1 reduce-scatter.10
  251.2 27.0 reduce-scatter.12
  282.9 132.3 reduce-scatter.8
where the time goes:
time: 544 us; the launch traced here: 539 us
  blocking collectives  332 us (61%)
  waiting for transfers between devices  69.5 us (13%)
  local copies, waits for them, and re-layouts  38.7 us (7%)
  starting transfers between devices  37.7 us (7%)
  matrix products  29.4 us (5%)
  other arithmetic  16.1 us (3%)
  between operations  16.1 us (3%)
    unnamed x1, blocking collectives  252 us
    psum x1, blocking collectives, body(): weight_sum = lax.psum(jnp.sum(sample_weight), ('tm', 'dp'))  79.7 us
    unnamed x5, waiting for transfers between devices  45.7 us
    unnamed x73, local copies, waits for them, and re-layouts  37.8 us
    ppermute x12, starting transfers between devices, shifted(): return lax.ppermute(x, axis, pairs)  37.3 us
    ppermute x12, waiting for transfers between devices, shifted(): return lax.ppermute(x, axis, pairs)  23.9 us
    dot_general x18, matrix products, outer_sum(): jnp.einsum('btc,btd->cd', left_op, right_op, preferred_element_type=jnp.f...  13.9 us
  transfers between devices with their start and end apart: 15, of which 13 were waited for; matrix products, arithmetic and copies ran while one was open for 8% of the time, Pallas kernels for 0%

commit v1 on v0

v1 whole, which is shorter than its diff:
```python
import functools

import jax
import jax.numpy as jnp
from jax import lax
from jax.experimental import pallas as pl
from jax.experimental.pallas import tpu as pltpu
from jax.sharding import PartitionSpec as P

MESH = pl.DeviceIdType.MESH
F32, BF16 = jnp.float32, jnp.bfloat16
C, LAYERS, T, HALO = 256, 6, 512, 64
EXT = T + 2 * HALO
POST = T + HALO
SIZES = {"x": 4, "y": 4, "z": 8}
BACK_ROWS = (544, 544, 544, 544, 544, 576)
PARTS = 9
ORDERS = ("yxz", "xyz", "zyx", "yxz", "xyz", "zyx", "yxz", "yxz", "xyz")

SCHEDULE = {
    5: (),
    4: (),
    3: ((0, 0),),
    2: ((1, 0), (2, 0)),
    1: ((3, 0), (0, 1), (1, 1), (2, 1)),
    0: (
        (4, 0), (5, 0), (6, 0), (3, 1), (0, 2), (1, 2), (2, 2), (4, 1), (5, 1), (7, 0), (8, 0), (6, 1), (3, 2),
        (4, 2), (5, 2), (7, 1), (8, 1), (6, 2), (7, 2), (8, 2),
    ),
}


def contract_rows(left, right):
    return lax.dot_general(left, right, (((0,), (0,)), ((), ())), preferred_element_type=F32)


def contract_columns(left, right):
    return lax.dot_general(left, right, (((1,), (1,)), ((), ())), preferred_element_type=F32)


def place():
    tm, y = lax.axis_index("tm"), lax.axis_index("dp")
    return {"x": tm // 16, "y": y, "z": (tm // 2) % 8, "core": tm % 2}


def device(at):
    return ((at["x"] * 8 + at["z"]) * 2 + at["core"], at["y"])


def peer(at, axis, step):
    if axis == "core":
        return dict(at, core=1 - at["core"])
    return dict(at, **{axis: (at[axis] + step) % SIZES[axis]})


def remote(src, dst, send, recv, target):
    copy = pltpu.make_async_remote_copy(
        src_ref=src, dst_ref=dst, send_sem=send, recv_sem=recv,
        device_id=target, device_id_type=MESH,
    )
    copy.start()
    return copy


def kernel(
    x_hbm, gso_hbm, gsk_hbm, sw_hbm, conv_hbm, outw_hbm,
    gin_ref, gconv_ref, gout_ref,
    xe, gse, gke, swe, conv, outw,
    stream, pres_s, gated_s, filt_s, open_s,
    gs, gproj, gp, gpb, later_b, mg, og,
    csend, crecv, hsum, wtile, wrecv,
    load_sem, halo_send, halo_recv, w_send, w_recv, p_send, p_recv, *rest,
):
    landings, sums = rest[:3 * PARTS], rest[3 * PARTS:]
    at = place()
    tm = lax.axis_index("tm")
    me = device(at)
    nxt = ((tm + 1) % 64, at["y"])
    prv = ((tm + 63) % 64, at["y"])

    barrier = pltpu.get_barrier_semaphore()
    greet = [nxt, prv, device(peer(at, "core", 1))]
    for axis in "yxz":
        greet += [device(peer(at, axis, k)) for k in range(1, SIZES[axis])]
    for target in greet:
        pl.semaphore_signal(barrier, inc=1, device_id=target, device_id_type=MESH)

    loads = [
        pltpu.make_async_copy(x_hbm.at[0], xe.at[pl.ds(HALO, T)], load_sem.at[0]),
        pltpu.make_async_copy(sw_hbm, swe.at[:, pl.ds(0, T)], load_sem.at[1]),
    ]
    for l in range(LAYERS):
        loads.append(pltpu.make_async_copy(conv_hbm.at[l], conv.at[l], load_sem.at[4 + l]))
        loads.append(pltpu.make_async_copy(outw_hbm.at[l], outw.at[l], load_sem.at[10 + l]))
    loads.append(pltpu.make_async_copy(gso_hbm.at[0], gse.at[pl.ds(0, T)], load_sem.at[2]))
    loads.append(pltpu.make_async_copy(gsk_hbm.at[0], gke.at[pl.ds(0, T)], load_sem.at[3]))
    for copy in loads:
        copy.start()
    pl.semaphore_wait(barrier, len(greet))

    halo = [
        remote(x_hbm.at[0, pl.ds(T - HALO, HALO)], xe.at[pl.ds(0, HALO)], halo_send.at[0], halo_recv.at[0], nxt),
        remote(x_hbm.at[0, pl.ds(0, HALO)], xe.at[pl.ds(HALO + T, HALO)], halo_send.at[1], halo_recv.at[1], prv),
        remote(gso_hbm.at[0, pl.ds(0, HALO)], gse.at[pl.ds(T, HALO)], halo_send.at[2], halo_recv.at[2], prv),
        remote(gsk_hbm.at[0, pl.ds(0, HALO)], gke.at[pl.ds(T, HALO)], halo_send.at[3], halo_recv.at[3], prv),
        remote(sw_hbm.at[:, pl.ds(0, 128)], swe.at[:, pl.ds(T, 128)], halo_send.at[4], halo_recv.at[4], prv),
    ]
    loads[0].wait()
    loads[1].wait()

    wtile[0] = jnp.broadcast_to(
        swe[:, 0:128] + swe[:, 128:256] + swe[:, 256:384] + swe[:, 384:512], (8, 128)
    )
    wcopies = []

    def weight_send(step, axis, base):
        count = 2 if axis == "core" else SIZES[axis]
        group = []
        for k in range(1, count):
            group.append(remote(
                wtile.at[step], wrecv.at[base + k - 1], w_send.at[base + k - 1], w_recv.at[base + k - 1],
                device(peer(at, axis, k)),
            ))
        wcopies.append((group, step, base))

    def weight_sum():
        group, step, base = wcopies[-1]
        total = wtile[step]
        for k, copy in enumerate(group):
            copy.wait_recv()
            total = total + wrecv[base + k]
        wtile[step + 1] = total

    weight_send(0, "core", 0)
    weight_steps = {0: ("y", 1), 1: ("x", 4), 3: ("z", 7)}

    stream[0:32] = jnp.zeros((32, C), F32)
    halo[0].wait_recv()
    halo[1].wait_recv()
    stream[32:32 + EXT] = xe[...].astype(F32)

    @pl.when(tm == 0)
    def _():
        stream[32:32 + HALO] = jnp.zeros((HALO, C), F32)

    step_rows = EXT // 2
    for l in range(LAYERS):
        d = 2**l
        loads[2 + 2 * l].wait()
        loads[3 + 2 * l].wait()
        for r0 in (step_rows, 0):
            present = stream[32 + r0:32 + r0 + step_rows].astype(BF16)
            earlier = stream[32 + r0 - d:32 + r0 - d + step_rows].astype(BF16)
            preact = jnp.dot(present, conv[l, 0:C], preferred_element_type=F32) + jnp.dot(
                earlier, conv[l, C:2 * C], preferred_element_type=F32
            )
            filtered = jnp.tanh(preact[:, :C])
            opening = 0.5 * jnp.tanh(0.5 * preact[:, C:]) + 0.5
            gated = (filtered * opening).astype(BF16)
            lo, hi = max(r0, HALO), r0 + step_rows
            filt_s[l, lo - HALO:hi - HALO] = filtered[lo - r0:]
            open_s[l, lo - HALO:hi - HALO] = opening[lo - r0:]
            own_hi = min(hi, HALO + T)
            pres_s[l, lo - HALO:own_hi - HALO] = present[lo - r0:own_hi - r0]
            gated_s[l, lo - HALO:own_hi - HALO] = gated[lo - r0:own_hi - r0]
            if l < LAYERS - 1:
                stream[32 + r0:32 + r0 + step_rows] += jnp.dot(
                    gated, outw[l, :, 0:C], preferred_element_type=F32
                )
        if l in weight_steps:
            weight_sum()
            weight_send(len(wcopies), *weight_steps[l])
    weight_sum()

    total = jnp.sum(wtile[4][0:1], axis=1, keepdims=True)
    scale = (64.0 * 4.0 * T) / total
    loads[-2].wait()
    loads[-1].wait()
    for i in (2, 3, 4):
        halo[i].wait_recv()
    last = tm == 63
    for b in range(5):
        rows = 128 if b < 4 else HALO
        lo = 128 * b
        weighting = jnp.broadcast_to(swe[:, lo:lo + 128] * scale, (128, 128)).T[:rows]
        if b == 4:
            weighting = jnp.where(last, 0.0, weighting)
        weighting = jnp.concatenate([weighting, weighting], axis=1)
        gs[lo:lo + rows] = gse[lo:lo + rows].astype(F32) * weighting
        gproj[lo:lo + rows, C:2 * C] = (gke[lo:lo + rows].astype(F32) * weighting).astype(BF16)

    copies = []
    pending = []

    def part_start(part, source):
        for half in range(2):
            for y in range(4):
                if part % 3 == 2:
                    if half == 1:
                        continue
                    tile = source[1 - at["core"], :, :, y * 128:(y + 1) * 128]
                    csend[part, y] = tile.reshape(4, 8, 8, 128).astype(BF16)
                else:
                    lo = (half * 4 + y) * 128
                    tile = source[:, pl.ds(1 - at["core"], 1), :, lo:lo + 128]
                    csend[part, y, 2 * half:2 * half + 2] = tile.reshape(2, 8, 8, 128).astype(BF16)
        copy = remote(
            csend.at[part], crecv.at[part], p_send.at[part, 0], p_recv.at[part, 0], device(peer(at, "core", 1))
        )
        copies.append(copy)
        return copy

    def part_join(part, source, copy):
        copy.wait_recv()
        for half in range(2):
            for y in range(4):
                if part % 3 == 2:
                    if half == 1:
                        continue
                    tile = source[at["core"], :, :, y * 128:(y + 1) * 128].reshape(4, 8, 8, 128)
                    hsum[part, y] = (tile + crecv[part, y].astype(F32)).astype(BF16)
                else:
                    lo = (half * 4 + y) * 128
                    tile = source[:, pl.ds(at["core"], 1), :, lo:lo + 128].reshape(2, 8, 8, 128)
                    rows = slice(2 * half, 2 * half + 2)
                    hsum[part, y, rows] = (tile + crecv[part, y, rows].astype(F32)).astype(BF16)
        stage_send(part, 0)

    def pick(ref, dims, axis, index):
        return ref.at[tuple(index if a == axis else slice(None) for a in dims)]

    def buffers(part, step):
        dims = [a for a in "yxz" if a not in ORDERS[part][:step]]
        source = hsum.at[part] if step == 0 else sums[2 * part + step - 1]
        return source, dims, landings[3 * part + step]

    def stage_send(part, step):
        axis = ORDERS[part][step]
        source, dims, landing = buffers(part, step)
        base = 1 + sum(SIZES[a] - 1 for a in ORDERS[part][:step])
        group = []
        for k in range(1, SIZES[axis]):
            other = peer(at, axis, k)
            copy = remote(
                pick(source, dims, axis, other[axis]), landing.at[k - 1],
                p_send.at[part, base + k - 1], p_recv.at[part, base + k - 1], device(other),
            )
            copies.append(copy)
            group.append(copy)
        pending.append((part, step, group))

    def stage_finish(part, step):
        entry = [e for e in pending if e[:2] == (part, step)][0]
        pending.remove(entry)
        axis = ORDERS[part][step]
        source, dims, landing = buffers(part, step)
        for copy in entry[2]:
            copy.wait_recv()
        total = pick(source, dims, axis, at[axis])[...].astype(F32)
        for k in range(SIZES[axis] - 1):
            total = total + landing[k].astype(F32)
        if step < 2:
            target, _, _ = buffers(part, step + 1)
            target[...] = total.astype(BF16)
            stage_send(part, step + 1)
        elif part % 3 == 2:
            high = LAYERS - 1 - 2 * (part // 3)
            gout_ref[high] = total[0:4]
            gout_ref[high - 1] = total[4:8]
        else:
            gconv_ref[LAYERS - 1 - 2 * (part // 3) - part % 3] = total

    gp[576:608] = jnp.zeros((32, 2 * C), F32)
    upper = lax.broadcasted_iota(jnp.int32, (32, 8, 2 * C), 1) < 4
    started = {}
    for l in reversed(range(LAYERS)):
        d = 2**l
        rows = BACK_ROWS[l]
        half_rows = 304 if rows > 560 else 272
        for r0, r1 in ((0, half_rows), (half_rows, rows)):
            gproj[r0:r1, 0:C] = gs[r0:r1].astype(BF16)
            grad_gated = contract_columns(gproj[r0:r1], outw[l])
            filtered, opening = filt_s[l, r0:r1], open_s[l, r0:r1]
            through = grad_gated * opening
            gp[r0:r1, 0:C] = through * (1.0 - filtered * filtered)
            gp[r0:r1, C:2 * C] = through * filtered * (1.0 - opening)
        pair = (LAYERS - 1 - l) // 2
        og[l % 2] = contract_rows(gated_s[l], gproj[0:T]).reshape(32, 8, 2 * C)
        if l % 2 == 0:
            high, low = og[1], og[0]
            shifted_low = pltpu.roll(low.reshape(256, 2 * C), 4, 0).reshape(32, 8, 2 * C)
            og2 = jnp.where(upper, high, shifted_low)
            shifted_high = pltpu.roll(high.reshape(256, 2 * C), 252, 0).reshape(32, 8, 2 * C)
            og[0] = og2
            og[1] = jnp.where(upper, shifted_high, low)
            part = 3 * pair + 2
            started[part] = part_start(part, og)
        update = BACK_ROWS[l - 1] if l else T
        gpb[0:rows] = gp[0:rows].astype(BF16)
        later_b[0:update] = gp[d:d + update].astype(BF16)
        part = 3 * pair + (1 - l % 2)
        mg[:, :, :, 0:2 * C] = contract_rows(pres_s[l], gpb[0:T]).reshape(16, 2, 8, 2 * C)
        mg[:, :, :, 2 * C:4 * C] = contract_rows(pres_s[l], later_b[0:T]).reshape(16, 2, 8, 2 * C)
        copy = part_start(part, mg)
        for r0, r1 in ((0, 256), (256, update)):
            taps = contract_columns(gpb[r0:r1], conv[l, 0:C]) + contract_columns(
                later_b[r0:r1], conv[l, C:2 * C]
            )
            grad_next = taps + gs[r0:r1]
            if l:
                gs[r0:r1] = grad_next
            else:
                gin_ref[0, r0:r1] = grad_next
        part_join(part, mg, copy)
        if l % 2 == 0:
            part_join(3 * pair + 2, og, started[3 * pair + 2])
        for part, step in SCHEDULE[l]:
            stage_finish(part, step)

    for copy in halo:
        copy.wait_send()
    for group, _, _ in wcopies:
        for copy in group:
            copy.wait_send()
    for copy in copies:
        copy.wait_send()


def body(inputs, grad_stream_out, grad_skip_out, sample_weight, conv_weight, out_weight):
    any_spec = pl.BlockSpec(memory_space=pl.ANY)
    vmem_spec = pl.BlockSpec(memory_space=pltpu.VMEM)
    landings, sums = [], []
    for order in ORDERS:
        for step in range(3):
            rest = tuple(SIZES[a] for a in "yxz" if a not in order[:step + 1])
            landings.append(pltpu.VMEM((SIZES[order[step]] - 1,) + rest + (8, 128), BF16))
            if step < 2:
                sums.append(pltpu.VMEM(rest + (8, 128), BF16))
    part_shape = (PARTS, 4, 4, 8, 8, 128)
    return pl.pallas_call(
        kernel,
        name="cycle",
        out_shape=(
            jax.ShapeDtypeStruct((1, T, C), F32),
            jax.ShapeDtypeStruct((LAYERS, 8, 128), F32),
            jax.ShapeDtypeStruct((LAYERS, 4, 128), F32),
        ),
        in_specs=[any_spec] * 6,
        out_specs=(vmem_spec, vmem_spec, vmem_spec),
        scratch_shapes=[
            pltpu.VMEM((EXT, C), BF16),
            pltpu.VMEM((POST, C), BF16),
            pltpu.VMEM((POST, C), BF16),
            pltpu.VMEM((1, T + 128), F32),
            pltpu.VMEM((LAYERS, 2 * C, 2 * C), BF16),
            pltpu.VMEM((LAYERS, C, 2 * C), BF16),
            pltpu.VMEM((32 + EXT, C), F32),
            pltpu.VMEM((LAYERS, T, C), BF16),
            pltpu.VMEM((LAYERS, T, C), BF16),
            pltpu.VMEM((LAYERS, POST, C), F32),
            pltpu.VMEM((LAYERS, POST, C), F32),
            pltpu.VMEM((POST, C), F32),
            pltpu.VMEM((POST, 2 * C), BF16),
            pltpu.VMEM((POST + 32, 2 * C), F32),
            pltpu.VMEM((POST, 2 * C), BF16),
            pltpu.VMEM((POST, 2 * C), BF16),
            pltpu.VMEM((16, 2, 8, 4 * C), F32),
            pltpu.VMEM((2, 32, 8, 2 * C), F32),
            pltpu.VMEM(part_shape, BF16),
            pltpu.VMEM(part_shape, BF16),
            pltpu.VMEM(part_shape, BF16),
            pltpu.VMEM((5, 8, 128), F32),
            pltpu.VMEM((14, 8, 128), F32),
            pltpu.SemaphoreType.DMA((16,)),
            pltpu.SemaphoreType.DMA((5,)),
            pltpu.SemaphoreType.DMA((5,)),
            pltpu.SemaphoreType.DMA((14,)),
            pltpu.SemaphoreType.DMA((14,)),
            pltpu.SemaphoreType.DMA((PARTS, 14)),
            pltpu.SemaphoreType.DMA((PARTS, 14)),
            *landings,
            *sums,
        ],
        compiler_params=pltpu.CompilerParams(
            collective_id=0, has_side_effects=True, vmem_limit_bytes=58 << 20
        ),
        cost_estimate=pl.CostEstimate(flops=8 * 10**9, bytes_accessed=8 * 10**6, transcendentals=4 * 10**6),
    )(inputs, grad_stream_out, grad_skip_out, sample_weight, conv_weight, out_weight)


def solution(mesh):
    placed = (
        P("dp", "tm", None),
        P("dp", "tm", None),
        P("dp", "tm", None),
        P("dp", "tm"),
        P(),
        P(),
    )
    return jax.shard_map(
        body,
        mesh=mesh,
        in_specs=placed,
        out_specs=(P("dp", "tm", None), P(None, "tm", "dp"), P(None, "tm", "dp")),
        check_vma=False,
    )
```

time: 544 us -> 69 us (0.13)
  blocking collectives: 332 us -> 0 us
  waiting for transfers between devices: 69.5 us -> 0 us
  Pallas kernels: 0 us -> 63.6 us
  starting transfers between devices: 37.7 us -> 0 us
  local copies, waits for them, and re-layouts: 38.7 us -> 4.52 us
  matrix products: 29.4 us -> 0 us
  other arithmetic: 16.1 us -> 0 us
  between operations: 16.1 us -> 0.64 us
    unnamed x1 -> x0, blocking collectives: 252 us -> none
    psum x1 -> x0, blocking collectives: 79.7 us -> none  [body(): weight_sum = lax.psum(jnp.sum(sample_weight), ('tm', 'dp'))]
    pallas_call x0 -> x1, Pallas kernels: none -> 63.6 us  [body(): pl.pallas_call(kernel, name='cycle', out_shape=(jax.ShapeDtypeStruct((1,...]
    unnamed x5 -> x0, waiting for transfers between devices: 45.7 us -> none
    ppermute x12 -> x0, starting transfers between devices: 37.3 us -> none  [shifted(): return lax.ppermute(x, axis, pairs)]
    unnamed x73 -> x3, local copies, waits for them, and re-layouts: 37.8 us -> 4.52 us
    dot_general x53 -> x0, matrix products: 29.4 us -> none  [the longest x18 13.9 us: outer_sum(): jnp.einsum('btc,btd->cd', left_op, right_op, preferred_element_type=jnp.f...]
    ppermute x12 -> x0, waiting for transfers between devices: 23.9 us -> none  [shifted(): return lax.ppermute(x, axis, pairs)]
  transfers between devices with their start and end apart: 15 -> 0, of which waited for: 13 -> 0; matrix products, arithmetic and copies ran while one was open for 8% -> 0% of each run, Pallas kernels for 0% -> 0%
where the time goes in v1:
time: 69 us; the launch traced here: 68.8 us
  Pallas kernels  63.6 us (92%)
  local copies, waits for them, and re-layouts  4.52 us (7%)
    pallas_call x1, Pallas kernels, body(): pl.pallas_call(kernel, name='cycle', out_shape=(jax.ShapeDtypeStruct((1,...  63.6 us
    unnamed x3, local copies, waits for them, and re-layouts  4.52 us

profile of v1, /device:TPU:1, one launch (start us, length us, event | category | flops | bytes accessed | tf_op | source)
XLA Modules:
  0.0 68.8 jit_solution(18109270622392320881)
XLA Ops:
  0.6 63.6 %cycle.1 = (f32[1,512,256]{2,1,0:T(8,128)}, f32[6,8,128]{2,1,0:T(8,128)}, f32[6,4,128]{2,1,0:T(4,128)}) custom-call(bf16[1,512,256]{2,1,0:T(8,128)(2,1)} %x_hbm.1, bf16[1,512,256]{2,1,0:T(8,128)(2,1)} %gso_hbm.1, bf16[1,512,256]{2,1,0:T(8,128)(2,1)} %gsk_hbm.1, f32[1,512]{1,0:T(1,128)} %sw_hbm.1, bf16[6,512,512]{2,1,0:T(8,128)(2,1)} %conv_hbm.1, ...), custom_call_target="tpu_custom_call" | custom-call | flops 8000000000 | bytes 8000000 | tf_op jit(solution)/shard_map/cycle/pallas_call | solution.py:340
  64.2 1.9 %copy.12 = f32[1,512,256]{2,1,0:T(8,128)} copy(f32[1,512,256]{2,1,0:T(8,128)} %get-tuple-element.6) | data formatting | bytes 1048576
  66.1 1.3 %copy.13 = f32[6,8,128]{2,1,0:T(8,128)} copy(f32[6,8,128]{2,1,0:T(8,128)} %get-tuple-element.7) | data formatting | bytes 49152
  67.5 1.3 %copy.14 = f32[6,4,128]{2,1,0:T(4,128)} copy(f32[6,4,128]{2,1,0:T(4,128)} %get-tuple-element.8) | data formatting | bytes 24576

commit v2 on v1

v2 whole, which is shorter than its diff:
```python
import functools

import jax
import jax.numpy as jnp
from jax import lax
from jax.experimental import pallas as pl
from jax.experimental.pallas import tpu as pltpu
from jax.sharding import PartitionSpec as P

MESH = pl.DeviceIdType.MESH
F32, BF16 = jnp.float32, jnp.bfloat16
C, LAYERS, T, HALO = 256, 6, 512, 64
EXT = T + 2 * HALO
POST = T + HALO
SIZES = {"x": 4, "y": 4, "z": 8}
BACK_ROWS = (544, 544, 544, 544, 544, 576)
START = (0, 0, 0, 16, 32, 64)
FIRST = (80, 96, 112, 128, 144, 176)
MIDDLE = 336
BARRIER_AFTER = 3
PARTS = 9
ORDERS = ("yxz", "xyz", "zyx", "yxz", "xyz", "zyx", "yxz", "yxz", "xyz")

GROUPS = ((0, 1, 3, 4), (6, 7, 8), (2, 5))
TAIL = (
    (0, 0), (1, 0), (3, 0), (4, 0), (0, 1), (1, 1), (6, 0), (8, 0), (2, 0), (3, 1), (4, 1), "g0",
    (7, 0), (6, 1), (8, 1), (2, 1), (5, 0), (7, 1), "g1", (5, 1), "g2", "e0", "e1", "e2",
)


def contract_rows(left, right):
    return lax.dot_general(left, right, (((0,), (0,)), ((), ())), preferred_element_type=F32)


def contract_columns(left, right):
    return lax.dot_general(left, right, (((1,), (1,)), ((), ())), preferred_element_type=F32)


def place():
    tm, y = lax.axis_index("tm"), lax.axis_index("dp")
    return {"x": tm // 16, "y": y, "z": (tm // 2) % 8, "core": tm % 2}


def device(at):
    return ((at["x"] * 8 + at["z"]) * 2 + at["core"], at["y"])


def peer(at, axis, step):
    if axis == "core":
        return dict(at, core=1 - at["core"])
    return dict(at, **{axis: (at[axis] + step) % SIZES[axis]})


def remote(src, dst, send, recv, target):
    copy = pltpu.make_async_remote_copy(
        src_ref=src, dst_ref=dst, send_sem=send, recv_sem=recv,
        device_id=target, device_id_type=MESH,
    )
    copy.start()
    return copy


def kernel(
    x_hbm, gso_hbm, gsk_hbm, sw_hbm, conv_hbm, outw_hbm,
    gin_hbm, parts_ref,
    xe, gse, gke, swe, conv, outw,
    stream, tail_s, postb, pres_s, gated_s, filt_s, open_s,
    gs, gproj, gp, gpb, later_b, mg, og,
    csend, crecv, hsum, wtile, wrecv,
    load_sem, halo_send, halo_recv, w_send, w_recv, c_send, c_recv, s_send, s_recv, g_send, g_recv, out_sem, *rest,
):
    landings, sums, finals, final_in = rest[:18], rest[18:27], rest[27:30], rest[30:]
    at = place()
    tm = lax.axis_index("tm")
    nxt = ((tm + 1) % 64, at["y"])
    prv = ((tm + 63) % 64, at["y"])

    barrier = pltpu.get_barrier_semaphore()
    greet = [nxt, prv, device(peer(at, "core", 1))]
    for axis in "yxz":
        greet += [device(peer(at, axis, k)) for k in range(1, SIZES[axis])]
    for target in greet:
        pl.semaphore_signal(barrier, inc=1, device_id=target, device_id_type=MESH)

    loads = [
        pltpu.make_async_copy(x_hbm.at[0], xe.at[pl.ds(HALO, T)], load_sem.at[0]),
        pltpu.make_async_copy(sw_hbm, swe.at[:, pl.ds(0, T)], load_sem.at[1]),
    ]
    for l in range(LAYERS):
        loads.append(pltpu.make_async_copy(conv_hbm.at[l], conv.at[l], load_sem.at[4 + l]))
        loads.append(pltpu.make_async_copy(outw_hbm.at[l], outw.at[l], load_sem.at[10 + l]))
    loads.append(pltpu.make_async_copy(gso_hbm.at[0], gse.at[pl.ds(0, T)], load_sem.at[2]))
    loads.append(pltpu.make_async_copy(gsk_hbm.at[0], gke.at[pl.ds(0, T)], load_sem.at[3]))
    for copy in loads:
        copy.start()

    def activate(l, present, earlier):
        preact = jnp.dot(present, conv[l, 0:C], preferred_element_type=F32) + jnp.dot(
            earlier, conv[l, C:2 * C], preferred_element_type=F32
        )
        filtered = jnp.tanh(preact[:, :C])
        opening = 0.5 * jnp.tanh(0.5 * preact[:, C:]) + 0.5
        return filtered, opening, (filtered * opening).astype(BF16)

    loads[0].wait()
    stream[32 + HALO:32 + HALO + T] = xe[HALO:HALO + T].astype(F32)
    wcopies = []
    halo = []
    for l in range(LAYERS):
        d = 2**l
        loads[2 + 2 * l].wait()
        loads[3 + 2 * l].wait()
        tail_s[l] = stream[HALO + T:HALO + T + 32]
        for lo, hi in ((MIDDLE, HALO + T), (FIRST[l], MIDDLE)):
            present = stream[32 + lo:32 + hi].astype(BF16)
            filtered, opening, gated = activate(l, present, stream[32 + lo - d:32 + hi - d].astype(BF16))
            filt_s[l, lo - HALO:hi - HALO] = filtered
            open_s[l, lo - HALO:hi - HALO] = opening
            pres_s[l, lo - HALO:hi - HALO] = present
            gated_s[l, lo - HALO:hi - HALO] = gated
            if l < LAYERS - 1:
                stream[32 + lo:32 + hi] += jnp.dot(gated, outw[l, :, 0:C], preferred_element_type=F32)
        if l == BARRIER_AFTER:
            pl.semaphore_wait(barrier, len(greet))
            first, final = pl.ds(0, HALO), pl.ds(T, HALO)
            halo = [
                remote(x_hbm.at[0, pl.ds(T - HALO, HALO)], xe.at[first], halo_send.at[0], halo_recv.at[0], nxt),
                remote(x_hbm.at[0, first], xe.at[pl.ds(HALO + T, HALO)], halo_send.at[1], halo_recv.at[1], prv),
                remote(gso_hbm.at[0, first], gse.at[final], halo_send.at[2], halo_recv.at[2], prv),
                remote(gsk_hbm.at[0, first], gke.at[final], halo_send.at[3], halo_recv.at[3], prv),
                remote(sw_hbm.at[:, pl.ds(0, 128)], swe.at[:, pl.ds(T, 128)], halo_send.at[4], halo_recv.at[4], prv),
            ]

    loads[1].wait()
    wtile[0] = jnp.broadcast_to(
        swe[:, 0:128] + swe[:, 128:256] + swe[:, 256:384] + swe[:, 384:512], (8, 128)
    )

    def weight_send(step, axis, base):
        group = []
        for k in range(1, 2 if axis == "core" else SIZES[axis]):
            slot = base + k - 1
            group.append(remote(
                wtile.at[step], wrecv.at[slot], w_send.at[slot], w_recv.at[slot], device(peer(at, axis, k))
            ))
        wcopies.append((group, step, base))

    def weight_sum():
        group, step, base = wcopies[-1]
        total = wtile[step]
        for k, copy in enumerate(group):
            copy.wait_recv()
            total = total + wrecv[base + k]
        wtile[step + 1] = total

    weight_send(0, "core", 0)

    loads[-2].wait()
    loads[-1].wait()

    def weigh(b, rows):
        lo = 128 * b
        weighting = jnp.broadcast_to(swe[:, lo:lo + 128], (128, 128)).T[:rows]
        if lo == T:
            weighting = jnp.where(tm == 63, 0.0, weighting)
        weighting = jnp.concatenate([weighting, weighting], axis=1)
        gs[lo:lo + rows] = gse[lo:lo + rows].astype(F32) * weighting
        gproj[lo:lo + rows, C:2 * C] = (gke[lo:lo + rows].astype(F32) * weighting).astype(BF16)

    for b in range(4):
        weigh(b, 128)

    stream[0:32] = jnp.zeros((32, C), F32)
    halo[0].wait_recv()
    halo[1].wait_recv()
    stream[32:32 + HALO] = jnp.where(tm == 0, 0.0, xe[0:HALO].astype(F32))
    postb[32:96] = xe[HALO + T:].astype(F32)
    for l in range(LAYERS):
        d = 2**l
        lo, hi = START[l], FIRST[l]
        count = hi - lo
        postb[0:32] = tail_s[l]
        present = jnp.concatenate([stream[32 + lo:32 + hi], postb[32:96]], axis=0).astype(BF16)
        earlier = jnp.concatenate([stream[32 + lo - d:32 + hi - d], postb[32 - d:96 - d]], axis=0).astype(BF16)
        filtered, opening, gated = activate(l, present, earlier)
        skip = HALO - lo
        filt_s[l, 0:hi - HALO] = filtered[skip:count]
        open_s[l, 0:hi - HALO] = opening[skip:count]
        pres_s[l, 0:hi - HALO] = present[skip:count]
        gated_s[l, 0:hi - HALO] = gated[skip:count]
        filt_s[l, T:POST] = filtered[count:]
        open_s[l, T:POST] = opening[count:]
        if l < LAYERS - 1:
            projected = jnp.dot(gated, outw[l, :, 0:C], preferred_element_type=F32)
            stream[32 + lo:32 + hi] += projected[:count]
            postb[32:96] += projected[count:]
        if l == 1:
            weight_sum()
            weight_send(1, "y", 1)
    for i in (2, 3, 4):
        halo[i].wait_recv()
    weigh(4, HALO)

    copies = []
    pending = []

    def part_start(part, source):
        for half in range(2):
            for y in range(4):
                if part % 3 == 2:
                    if half == 1:
                        continue
                    tile = source[1 - at["core"], :, :, y * 128:(y + 1) * 128]
                    csend[part, y] = tile.reshape(4, 8, 8, 128).astype(BF16)
                else:
                    lo = (half * 4 + y) * 128
                    tile = source[:, pl.ds(1 - at["core"], 1), :, lo:lo + 128]
                    csend[part, y, 2 * half:2 * half + 2] = tile.reshape(2, 8, 8, 128).astype(BF16)
        copy = remote(
            csend.at[part], crecv.at[part], c_send.at[part], c_recv.at[part], device(peer(at, "core", 1))
        )
        copies.append(copy)
        return copy

    def part_join(part, source, copy):
        copy.wait_recv()
        for half in range(2):
            for y in range(4):
                if part % 3 == 2:
                    if half == 1:
                        continue
                    tile = source[at["core"], :, :, y * 128:(y + 1) * 128].reshape(4, 8, 8, 128)
                    hsum[part, y] = (tile + crecv[part, y].astype(F32)).astype(BF16)
                else:
                    lo = (half * 4 + y) * 128
                    tile = source[:, pl.ds(at["core"], 1), :, lo:lo + 128].reshape(2, 8, 8, 128)
                    rows = slice(2 * half, 2 * half + 2)
                    hsum[part, y, rows] = (tile + crecv[part, y, rows].astype(F32)).astype(BF16)
        stage_send(part, 0)

    def pick(ref, dims, axis, index):
        return ref.at[tuple(index if a == axis else slice(None) for a in dims)]

    def send_all(axis, pick_source, landing, send, recv):
        for k in range(1, SIZES[axis]):
            other = peer(at, axis, k)
            remote(pick_source(other[axis]), landing.at[k - 1], send, recv, device(other))
        waits.append((landing, send))

    def wait_all(landing, semaphore):
        pltpu.make_async_copy(landing, landing, semaphore).wait()

    def stage(part, step):
        dims = [a for a in "yxz" if a not in ORDERS[part][:step]]
        source = hsum.at[part] if step == 0 else sums[part]
        return ORDERS[part][step], dims, source, landings[2 * part + step]

    def stage_send(part, step):
        axis, dims, source, landing = stage(part, step)
        send_all(axis, lambda i: pick(source, dims, axis, i), landing, s_send.at[part, step], s_recv.at[part, step])

    def stage_finish(part, step):
        axis, dims, source, landing = stage(part, step)
        wait_all(landing, s_recv.at[part, step])
        total = pick(source, dims, axis, at[axis])[...].astype(F32)
        for k in range(SIZES[axis] - 1):
            total = total + landing[k].astype(F32)
        if step == 0:
            sums[part][...] = total.astype(BF16)
            stage_send(part, 1)
        else:
            g = [part in group for group in GROUPS].index(True)
            finals[g][:, GROUPS[g].index(part)] = total.astype(BF16)

    def group_send(g):
        send_all(ORDERS[GROUPS[g][0]][2], lambda i: finals[g].at[i], final_in[g], g_send.at[g], g_recv.at[g])

    def group_finish(g, scale):
        axis = ORDERS[GROUPS[g][0]][2]
        wait_all(final_in[g], g_recv.at[g])
        total = finals[g][at[axis]].astype(F32)
        for k in range(SIZES[axis] - 1):
            total = total + final_in[g][k].astype(F32)
        for j, part in enumerate(GROUPS[g]):
            parts_ref[part] = total[j] * scale

    waits = []
    gp[576:608] = jnp.zeros((32, 2 * C), F32)
    upper = lax.broadcasted_iota(jnp.int32, (32, 8, 2 * C), 1) < 4
    joins = []
    for l in reversed(range(LAYERS)):
        d = 2**l
        rows = BACK_ROWS[l]
        half_rows = 304 if rows > 560 else 272
        for r0, r1 in ((0, half_rows), (half_rows, rows)):
            gproj[r0:r1, 0:C] = gs[r0:r1].astype(BF16)
            grad_gated = contract_columns(gproj[r0:r1], outw[l])
            filtered, opening = filt_s[l, r0:r1], open_s[l, r0:r1]
            through = grad_gated * opening
            gp[r0:r1, 0:C] = through * (1.0 - filtered * filtered)
            gp[r0:r1, C:2 * C] = through * filtered * (1.0 - opening)
        for join in joins:
            part_join(*join)
        joins = []
        pair = (LAYERS - 1 - l) // 2
        update = BACK_ROWS[l - 1] if l else T
        gpb[0:rows] = gp[0:rows].astype(BF16)
        later_b[0:update] = gp[d:d + update].astype(BF16)
        part = 3 * pair + (1 - l % 2)
        mg[:, :, :, 0:2 * C] = contract_rows(pres_s[l], gpb[0:T]).reshape(16, 2, 8, 2 * C)
        mg[:, :, :, 2 * C:4 * C] = contract_rows(pres_s[l], later_b[0:T]).reshape(16, 2, 8, 2 * C)
        joins.append((part, mg, part_start(part, mg)))
        og[l % 2] = contract_rows(gated_s[l], gproj[0:T]).reshape(32, 8, 2 * C)
        if l % 2 == 0:
            high, low = og[1], og[0]
            shifted_low = pltpu.roll(low.reshape(256, 2 * C), 4, 0).reshape(32, 8, 2 * C)
            shifted_high = pltpu.roll(high.reshape(256, 2 * C), 252, 0).reshape(32, 8, 2 * C)
            og[0] = jnp.where(upper, high, shifted_low)
            og[1] = jnp.where(upper, shifted_high, low)
            part = 3 * pair + 2
            joins.append((part, og, part_start(part, og)))
        for r0, r1 in ((0, 256), (256, update)):
            taps = contract_columns(gpb[r0:r1], conv[l, 0:C]) + contract_columns(
                later_b[r0:r1], conv[l, C:2 * C]
            )
            grad_next = taps + gs[r0:r1]
            gs[r0:r1] = grad_next
        if l == 5:
            weight_sum()
            weight_send(2, "x", 4)
        if l == 2:
            weight_sum()
            weight_send(3, "z", 7)
    for join in joins:
        part_join(*join)
    for item in TAIL:
        if item == "g0":
            group_send(0)
            weight_sum()
            scale = (64.0 * 4.0 * T) / jnp.sum(wtile[4][0:1], axis=1, keepdims=True)
            gs[0:T] = gs[0:T] * scale
            out_copy = pltpu.make_async_copy(gs.at[pl.ds(0, T)], gin_hbm.at[0], out_sem)
            out_copy.start()
        elif item in ("g1", "g2"):
            group_send(int(item[1]))
        elif item in ("e0", "e1", "e2"):
            group_finish(int(item[1]), scale)
        else:
            stage_finish(*item)
    out_copy.wait()
    for landing, semaphore in waits:
        wait_all(landing, semaphore)

    for copy in halo:
        copy.wait_send()
    for group, _, _ in wcopies:
        for copy in group:
            copy.wait_send()
    for copy in copies:
        copy.wait_send()


def deliver(gin_ref, parts_ref, gin_out, gconv_out, gout_out):
    gin_out[...] = gin_ref[...]
    for part in range(PARTS):
        layer = LAYERS - 1 - 2 * (part // 3)
        if part % 3 == 2:
            gout_out[layer] = parts_ref[part, 0:4]
            gout_out[layer - 1] = parts_ref[part, 4:8]
        else:
            gconv_out[layer - part % 3] = parts_ref[part]


def body(inputs, grad_stream_out, grad_skip_out, sample_weight, conv_weight, out_weight):
    any_spec = pl.BlockSpec(memory_space=pl.ANY)
    vmem_spec = pl.BlockSpec(memory_space=pltpu.VMEM)
    landings, sums, finals, final_in = [], [], [], []
    for order in ORDERS:
        for step in range(2):
            rest = tuple(SIZES[a] for a in "yxz" if a not in order[:step + 1])
            landings.append(pltpu.VMEM((SIZES[order[step]] - 1,) + rest + (8, 128), BF16))
            if step == 0:
                sums.append(pltpu.VMEM(rest + (8, 128), BF16))
    for group in GROUPS:
        size = SIZES[ORDERS[group[0]][2]]
        finals.append(pltpu.VMEM((size, len(group), 8, 128), BF16))
        final_in.append(pltpu.VMEM((size - 1, len(group), 8, 128), BF16))
    part_shape = (PARTS, 4, 4, 8, 8, 128)
    gin, parts = pl.pallas_call(
        kernel,
        name="cycle",
        out_shape=(
            jax.ShapeDtypeStruct((1, T, C), F32),
            jax.ShapeDtypeStruct((PARTS, 8, 128), F32),
        ),
        in_specs=[any_spec] * 6,
        out_specs=(any_spec, vmem_spec),
        scratch_shapes=[
            pltpu.VMEM((EXT, C), BF16),
            pltpu.VMEM((POST, C), BF16),
            pltpu.VMEM((POST, C), BF16),
            pltpu.VMEM((1, T + 128), F32),
            pltpu.VMEM((LAYERS, 2 * C, 2 * C), BF16),
            pltpu.VMEM((LAYERS, C, 2 * C), BF16),
            pltpu.VMEM((32 + HALO + T, C), F32),
            pltpu.VMEM((LAYERS, 32, C), F32),
            pltpu.VMEM((96, C), F32),
            pltpu.VMEM((LAYERS, T, C), BF16),
            pltpu.VMEM((LAYERS, T, C), BF16),
            pltpu.VMEM((LAYERS, POST, C), F32),
            pltpu.VMEM((LAYERS, POST, C), F32),
            pltpu.VMEM((POST, C), F32),
            pltpu.VMEM((POST, 2 * C), BF16),
            pltpu.VMEM((POST + 32, 2 * C), F32),
            pltpu.VMEM((POST, 2 * C), BF16),
            pltpu.VMEM((POST, 2 * C), BF16),
            pltpu.VMEM((16, 2, 8, 4 * C), F32),
            pltpu.VMEM((2, 32, 8, 2 * C), F32),
            pltpu.VMEM(part_shape, BF16),
            pltpu.VMEM(part_shape, BF16),
            pltpu.VMEM(part_shape, BF16),
            pltpu.VMEM((5, 8, 128), F32),
            pltpu.VMEM((14, 8, 128), F32),
            pltpu.SemaphoreType.DMA((16,)),
            pltpu.SemaphoreType.DMA((5,)),
            pltpu.SemaphoreType.DMA((5,)),
            pltpu.SemaphoreType.DMA((14,)),
            pltpu.SemaphoreType.DMA((14,)),
            pltpu.SemaphoreType.DMA((PARTS,)),
            pltpu.SemaphoreType.DMA((PARTS,)),
            pltpu.SemaphoreType.DMA((PARTS, 2)),
            pltpu.SemaphoreType.DMA((PARTS, 2)),
            pltpu.SemaphoreType.DMA((3,)),
            pltpu.SemaphoreType.DMA((3,)),
            pltpu.SemaphoreType.DMA,
            *landings,
            *sums,
            *finals,
            *final_in,
        ],
        compiler_params=pltpu.CompilerParams(
            collective_id=0, has_side_effects=True, vmem_limit_bytes=58 << 20
        ),
        cost_estimate=pl.CostEstimate(flops=8 * 10**9, bytes_accessed=8 * 10**6, transcendentals=4 * 10**6),
    )(inputs, grad_stream_out, grad_skip_out, sample_weight, conv_weight, out_weight)
    return pl.pallas_call(
        deliver,
        name="deliver",
        out_shape=(
            jax.ShapeDtypeStruct((1, T, C), F32),
            jax.ShapeDtypeStruct((LAYERS, 8, 128), F32),
            jax.ShapeDtypeStruct((LAYERS, 4, 128), F32),
        ),
        in_specs=[vmem_spec, vmem_spec],
        out_specs=(vmem_spec, vmem_spec, vmem_spec),
    )(gin, parts)


def solution(mesh):
    placed = (
        P("dp", "tm", None),
        P("dp", "tm", None),
        P("dp", "tm", None),
        P("dp", "tm"),
        P(),
        P(),
    )
    return jax.shard_map(
        body,
        mesh=mesh,
        in_specs=placed,
        out_specs=(P("dp", "tm", None), P(None, "tm", "dp"), P(None, "tm", "dp")),
        check_vma=False,
    )
```

time: 69 us -> 51.1 us (0.74)
  Pallas kernels: 63.6 us -> 49.8 us
  local copies, waits for them, and re-layouts: 4.52 us -> 0 us
    pallas_call x1, Pallas kernels: 63.6 us -> 47.9 us  [body(): pl.pallas_call(kernel, name='cycle', out_shape=(jax.ShapeDtypeStruct((1,...]
    unnamed x3 -> x0, local copies, waits for them, and re-layouts: 4.52 us -> none
    pallas_call x0 -> x1, Pallas kernels: none -> 1.88 us  [body(): pl.pallas_call(deliver, name='deliver', out_shape=(jax.ShapeDtypeStruct((...]
where the time goes in v2:
time: 51.1 us; the launch traced here: 50.4 us
  Pallas kernels  49.8 us (97%)
  between operations  0.64 us (1%)
    pallas_call x1, Pallas kernels, body(): pl.pallas_call(kernel, name='cycle', out_shape=(jax.ShapeDtypeStruct((1,...  47.9 us
    pallas_call x1, Pallas kernels, body(): pl.pallas_call(deliver, name='deliver', out_shape=(jax.ShapeDtypeStruct((...  1.88 us

profile of v2, /device:TPU:1, one launch (start us, length us, event | category | flops | bytes accessed | tf_op | source)
XLA Modules:
  0.0 50.4 jit_solution(5056896880988243007)
XLA Ops:
  0.6 47.9 %cycle.1 = (f32[1,512,256]{2,1,0:T(8,128)}, f32[9,8,128]{2,1,0:T(8,128)}) custom-call(bf16[1,512,256]{2,1,0:T(8,128)(2,1)} %x_hbm.1, bf16[1,512,256]{2,1,0:T(8,128)(2,1)} %gso_hbm.1, bf16[1,512,256]{2,1,0:T(8,128)(2,1)} %gsk_hbm.1, f32[1,512]{1,0:T(1,128)} %sw_hbm.1, bf16[6,512,512]{2,1,0:T(8,128)(2,1)} %conv_hbm.1, bf16[6,256,512]{2,1,0:T(8,128)(2,1)} %outw_hbm.1), custom_call_target="tpu_custom_call" | custom-call | flops 8000000000 | bytes 8000000 | tf_op jit(solution)/shard_map/cycle/pallas_call | solution.py:389
  48.6 1.9 %deliver.1 = (f32[1,512,256]{2,1,0:T(8,128)}, f32[6,8,128]{2,1,0:T(8,128)}, f32[6,4,128]{2,1,0:T(4,128)}) custom-call(f32[1,512,256]{2,1,0:T(8,128)} %get-tuple-element.5.gin_ref, f32[9,8,128]{2,1,0:T(8,128)} %get-tuple-element.6.parts_ref), custom_call_target="tpu_custom_call" | custom-call | tf_op jit(solution)/shard_map/deliver/pallas_call | solution.py:446

commit v3 on v2

v3 whole, which is shorter than its diff:
```python
import functools

import jax
import jax.numpy as jnp
from jax import lax
from jax.experimental import pallas as pl
from jax.experimental.pallas import tpu as pltpu
from jax.sharding import PartitionSpec as P

MESH = pl.DeviceIdType.MESH
F32, BF16 = jnp.float32, jnp.bfloat16
C, LAYERS, T, HALO = 256, 6, 512, 64
EXT = T + 2 * HALO
POST = T + HALO
SIZES = {"x": 4, "y": 4, "z": 8}
BACK_ROWS = (544, 544, 544, 544, 544, 576)
START = (0, 0, 0, 16, 32, 64)
FIRST = (80, 96, 112, 128, 144, 176)
MIDDLE = 336
BUFFERS = 17
CHUNKS = ((5,), (4, 3), (2, 1), (0,))
HALVED = (0, 1, 2)
INSIDE = {1: ((0, 0),)}
TAIL = (
    (1, 0), (0, 1), (2, 0), (1, 1), (0, 2), (3, 1), (2, 1), (1, 2), "scale", (0, 3), (3, 2), (2, 2), (1, 3), (3, 3),
    (2, 3),
)


def contract_rows(left, right):
    return lax.dot_general(left, right, (((0,), (0,)), ((), ())), preferred_element_type=F32)


def contract_columns(left, right):
    return lax.dot_general(left, right, (((1,), (1,)), ((), ())), preferred_element_type=F32)


def place():
    tm, y = lax.axis_index("tm"), lax.axis_index("dp")
    return {"x": tm // 16, "y": y, "z": (tm // 2) % 8, "core": tm % 2}


def device(at):
    return ((at["x"] * 8 + at["z"]) * 2 + at["core"], at["y"])


def flips(i):
    return (i + 1 - 2 * (i % 2), 3 - i), (3 - i, i + 1 - 2 * (i % 2))


def peer(at, axis, step):
    if axis == "core":
        return dict(at, core=1 - at["core"])
    return dict(at, **{axis: (at[axis] + step) % SIZES[axis]})


def remote(src, dst, send, recv, target):
    copy = pltpu.make_async_remote_copy(
        src_ref=src, dst_ref=dst, send_sem=send, recv_sem=recv,
        device_id=target, device_id_type=MESH,
    )
    copy.start()
    return copy


def kernel(
    x_hbm, gso_hbm, gsk_hbm, sw_hbm, conv_hbm, outw_hbm,
    gin_hbm, parts_ref,
    xe, gse, gke, swe, conv, outw,
    stream, tail_s, postb, pres_s, gated_s, filt_s, open_s,
    gs, gproj, gp, gpb, later_b, wtile, wrecv,
    load_sem, halo_send, halo_recv, w_send, w_recv, p_send, p_recv, out_sem, *rest,
):
    bufs = [rest[BUFFERS * i:BUFFERS * (i + 1)] for i in range(len(CHUNKS))]
    at = place()
    tm = lax.axis_index("tm")
    nxt = ((tm + 1) % 64, at["y"])
    prv = ((tm + 63) % 64, at["y"])

    barrier = pltpu.get_barrier_semaphore()
    greet = [nxt, prv, device(peer(at, "core", 1))]
    for axis in "yxz":
        greet += [device(peer(at, axis, k)) for k in range(1, SIZES[axis])]
    for target in greet:
        pl.semaphore_signal(barrier, inc=1, device_id=target, device_id_type=MESH)

    loads = [
        pltpu.make_async_copy(x_hbm.at[0], xe.at[pl.ds(HALO, T)], load_sem.at[0]),
        pltpu.make_async_copy(sw_hbm, swe.at[:, pl.ds(0, T)], load_sem.at[1]),
    ]
    for l in range(LAYERS):
        loads.append(pltpu.make_async_copy(conv_hbm.at[l], conv.at[l], load_sem.at[4 + l]))
        loads.append(pltpu.make_async_copy(outw_hbm.at[l], outw.at[l], load_sem.at[10 + l]))
    loads.append(pltpu.make_async_copy(gso_hbm.at[0], gse.at[pl.ds(0, T)], load_sem.at[2]))
    loads.append(pltpu.make_async_copy(gsk_hbm.at[0], gke.at[pl.ds(0, T)], load_sem.at[3]))
    for copy in loads[:6]:
        copy.start()

    pl.semaphore_wait(barrier, len(greet))
    first, final = pl.ds(0, HALO), pl.ds(T, HALO)
    halo = [
        remote(x_hbm.at[0, pl.ds(T - HALO, HALO)], xe.at[first], halo_send.at[0], halo_recv.at[0], nxt),
        remote(x_hbm.at[0, first], xe.at[pl.ds(HALO + T, HALO)], halo_send.at[1], halo_recv.at[1], prv),
        remote(gso_hbm.at[0, first], gse.at[final], halo_send.at[2], halo_recv.at[2], prv),
        remote(gsk_hbm.at[0, first], gke.at[final], halo_send.at[3], halo_recv.at[3], prv),
        remote(sw_hbm.at[:, pl.ds(0, 128)], swe.at[:, pl.ds(T, 128)], halo_send.at[4], halo_recv.at[4], prv),
    ]

    def activate(l, present, earlier):
        preact = jnp.dot(present, conv[l, 0:C], preferred_element_type=F32) + jnp.dot(
            earlier, conv[l, C:2 * C], preferred_element_type=F32
        )
        filtered = jnp.tanh(preact[:, :C])
        opening = 0.5 * jnp.tanh(0.5 * preact[:, C:]) + 0.5
        return filtered, opening, (filtered * opening).astype(BF16)

    loads[0].wait()
    stream[32 + HALO:32 + HALO + T] = xe[HALO:HALO + T].astype(F32)
    wcopies = []
    for l in range(LAYERS):
        d = 2**l
        loads[2 + 2 * l].wait()
        loads[3 + 2 * l].wait()
        for copy in loads[6 + 2 * l:8 + 2 * l]:
            copy.start()
        tail_s[l] = stream[HALO + T:HALO + T + 32]
        for lo, hi in ((MIDDLE, HALO + T), (FIRST[l], MIDDLE)):
            present = stream[32 + lo:32 + hi].astype(BF16)
            filtered, opening, gated = activate(l, present, stream[32 + lo - d:32 + hi - d].astype(BF16))
            filt_s[l, lo - HALO:hi - HALO] = filtered
            open_s[l, lo - HALO:hi - HALO] = opening
            pres_s[l, lo - HALO:hi - HALO] = present
            gated_s[l, lo - HALO:hi - HALO] = gated
            if l < LAYERS - 1:
                stream[32 + lo:32 + hi] += jnp.dot(gated, outw[l, :, 0:C], preferred_element_type=F32)

    loads[1].wait()
    wtile[0] = jnp.broadcast_to(
        swe[:, 0:128] + swe[:, 128:256] + swe[:, 256:384] + swe[:, 384:512], (8, 128)
    )

    def weight_send(step, axis, base):
        group = []
        for k in range(1, 2 if axis == "core" else SIZES[axis]):
            slot = base + k - 1
            group.append(remote(
                wtile.at[step], wrecv.at[slot], w_send.at[slot], w_recv.at[slot], device(peer(at, axis, k))
            ))
        wcopies.append((group, step, base))

    def weight_sum():
        group, step, base = wcopies[-1]
        total = wtile[step]
        for k, copy in enumerate(group):
            copy.wait_recv()
            total = total + wrecv[base + k]
        wtile[step + 1] = total

    weight_send(0, "core", 0)

    loads[-2].wait()
    loads[-1].wait()

    def weigh(b, rows):
        lo = 128 * b
        weighting = jnp.broadcast_to(swe[:, lo:lo + 128], (128, 128)).T[:rows]
        if lo == T:
            weighting = jnp.where(tm == 63, 0.0, weighting)
        weighting = jnp.concatenate([weighting, weighting], axis=1)
        gs[lo:lo + rows] = gse[lo:lo + rows].astype(F32) * weighting
        gproj[lo:lo + rows, C:2 * C] = (gke[lo:lo + rows].astype(F32) * weighting).astype(BF16)

    for b in range(4):
        weigh(b, 128)

    stream[0:32] = jnp.zeros((32, C), F32)
    halo[0].wait_recv()
    halo[1].wait_recv()
    stream[32:32 + HALO] = jnp.where(tm == 0, 0.0, xe[0:HALO].astype(F32))
    postb[32:96] = xe[HALO + T:].astype(F32)
    for l in range(LAYERS):
        d = 2**l
        lo, hi = START[l], FIRST[l]
        count = hi - lo
        postb[0:32] = tail_s[l]
        present = jnp.concatenate([stream[32 + lo:32 + hi], postb[32:96]], axis=0).astype(BF16)
        earlier = jnp.concatenate([stream[32 + lo - d:32 + hi - d], postb[32 - d:96 - d]], axis=0).astype(BF16)
        filtered, opening, gated = activate(l, present, earlier)
        skip = HALO - lo
        filt_s[l, 0:hi - HALO] = filtered[skip:count]
        open_s[l, 0:hi - HALO] = opening[skip:count]
        pres_s[l, 0:hi - HALO] = present[skip:count]
        gated_s[l, 0:hi - HALO] = gated[skip:count]
        filt_s[l, T:POST] = filtered[count:]
        open_s[l, T:POST] = opening[count:]
        if l < LAYERS - 1:
            projected = jnp.dot(gated, outw[l, :, 0:C], preferred_element_type=F32)
            stream[32 + lo:32 + hi] += projected[:count]
            postb[32:96] += projected[count:]
        if l == 1:
            weight_sum()
            weight_send(1, "y", 1)
    for i in (2, 3, 4):
        halo[i].wait_recv()
    weigh(4, HALO)

    waits = []

    def send_all(axis, pick_source, landing, send, recv):
        for k in range(1, SIZES[axis]):
            other = peer(at, axis, k)
            remote(pick_source(other[axis]), landing.at[k - 1], send, recv, device(other))
        waits.append((landing, send))

    def wait_all(landing, semaphore):
        pltpu.make_async_copy(landing, landing, semaphore).wait()

    def collect(own, landing):
        low = own.astype(F32) + landing[0].astype(F32)
        return low + (landing[1].astype(F32) + landing[2].astype(F32))

    def chunk_join(i):
        grads, other, held, y_in, x_in = bufs[i][:5]
        wait_all(other, p_recv.at[i, 0])
        held[...] = grads[at["core"]] + other[...]
        if i in HALVED:
            for k, axis in enumerate("yx"):
                for half, (target, _) in enumerate(flips(at[axis])):
                    for slot, block in enumerate((target, (at[axis] + 2) % 4)):
                        remote(
                            held.at[quarter(axis, block, half)], bufs[i][11 + k].at[half, slot],
                            p_send.at[i, 1 + k], p_recv.at[i, 1 + k], device(dict(at, **{axis: target})),
                        )
                waits.append((bufs[i][11 + k], p_send.at[i, 1 + k]))
            return
        send_all("y", lambda y: held.at[y, :, :, pl.ds(0, 3)], y_in, p_send.at[i, 1], p_recv.at[i, 1])
        send_all("x", lambda x: held.at[:, x, :, pl.ds(3, 3)], x_in, p_send.at[i, 2], p_recv.at[i, 2])

    def quarter(axis, block, half):
        rest = pl.ds(2 * half, 2)
        if axis == "y":
            return block, rest, slice(None), pl.ds(0, 3)
        return rest, block, slice(None), pl.ds(3, 3)

    def stage0(i):
        held = bufs[i][2]
        for k, axis in enumerate("yx"):
            arrived, kept, final_in = bufs[i][11 + k], bufs[i][13 + k], bufs[i][15 + k]
            wait_all(arrived, p_recv.at[i, 1 + k])
            for half, (_, target) in enumerate(flips(at[axis])):
                kept[half] = held[quarter(axis, target, half)] + arrived[half, 1]
                remote(
                    kept.at[half], final_in.at[half], p_send.at[i, 6 + k], p_recv.at[i, 6 + k],
                    device(dict(at, **{axis: target})),
                )
            waits.append((final_in, p_send.at[i, 6 + k]))

    def halved_sum(i, k):
        axis = "yx"[k]
        held, arrived, final_in, total = bufs[i][2], bufs[i][11 + k], bufs[i][15 + k], bufs[i][5 + k]
        wait_all(final_in, p_recv.at[i, 6 + k])
        for half in range(2):
            own = held[quarter(axis, at[axis], half)].astype(F32) + arrived[half, 0].astype(F32)
            total[2 * half:2 * half + 2] = (own + final_in[half].astype(F32)).astype(BF16)

    def stage1(i):
        held, y_in, x_in, y_sum, x_sum, yx_in, xy_in = bufs[i][2:9]
        if i in HALVED:
            halved_sum(i, 0)
        else:
            wait_all(y_in, p_recv.at[i, 1])
            y_sum[...] = collect(held[at["y"], :, :, 0:3], y_in).astype(BF16)
        send_all("x", lambda x: y_sum.at[x], yx_in, p_send.at[i, 3], p_recv.at[i, 3])
        if i in HALVED:
            halved_sum(i, 1)
        else:
            wait_all(x_in, p_recv.at[i, 2])
            x_sum[...] = collect(held[:, at["x"], :, 3:6], x_in).astype(BF16)
        send_all("y", lambda y: x_sum.at[y], xy_in, p_send.at[i, 4], p_recv.at[i, 4])

    mine = at["z"] // 4 == at["core"]

    def stage2(i):
        y_sum, x_sum, yx_in, xy_in, last_out, last_in = bufs[i][5:11]
        wait_all(yx_in, p_recv.at[i, 3])
        tiles = [collect(y_sum[at["x"]], yx_in)]
        wait_all(xy_in, p_recv.at[i, 4])
        tiles.append(collect(x_sum[at["y"]], xy_in))
        for j in range(4):
            rows = tiles[j // 3][:, j % 3]
            out_rows = tiles[1][:, 1 + j // 2, 8 * (j % 2):8 * (j % 2) + 8]
            for c in range(2):
                last_out[j, c] = jnp.concatenate([rows[:, 8 * c:8 * c + 8], out_rows], axis=1).astype(BF16)
        for j in range(4):
            for c in range(2):
                z = 4 * at["core"] + j
                here = jnp.logical_and(z == at["z"], c == at["core"])
                source, target = last_out.at[j, c], last_in.at[at["z"]]

                @pl.when(jnp.logical_not(here))
                def _():
                    remote(source, target, p_send.at[i, 5], p_recv.at[i, 5], device(dict(at, z=z, core=c)))

                @pl.when(here)
                def _():
                    pltpu.make_async_copy(source, target, p_recv.at[i, 5]).start()

    def stage3(i, scale):
        last_in = bufs[i][10]
        wait_all(last_in, p_recv.at[i, 5])
        total = last_in[0].astype(F32)
        for k in range(1, 8):
            total = total + last_in[k].astype(F32)
        total = total * scale
        for j, l in enumerate(CHUNKS[i]):
            parts_ref[l] = total[j]

    gp[576:608] = jnp.zeros((32, 2 * C), F32)
    joins = []
    for l in reversed(range(LAYERS)):
        d = 2**l
        rows = BACK_ROWS[l]
        half_rows = 304 if rows > 560 else 272
        for r0, r1 in ((0, half_rows), (half_rows, rows)):
            gproj[r0:r1, 0:C] = gs[r0:r1].astype(BF16)
            grad_gated = contract_columns(gproj[r0:r1], outw[l])
            filtered, opening = filt_s[l, r0:r1], open_s[l, r0:r1]
            through = grad_gated * opening
            gp[r0:r1, 0:C] = through * (1.0 - filtered * filtered)
            gp[r0:r1, C:2 * C] = through * filtered * (1.0 - opening)
        ready, joins = joins, []
        update = BACK_ROWS[l - 1] if l else T
        gpb[0:rows] = gp[0:rows].astype(BF16)
        later_b[0:update] = gp[d:d + update].astype(BF16)
        i = [l in chunk for chunk in CHUNKS].index(True)
        grads, j = bufs[i][0], CHUNKS[i].index(l)
        products = (
            contract_rows(pres_s[l], gpb[0:T]),
            contract_rows(pres_s[l], later_b[0:T]),
            contract_rows(gated_s[l], gproj[0:T]),
        )
        for half in range(2):
            for y in range(4):
                for k in range(2):
                    tile = products[k][:, y * 128:(y + 1) * 128].astype(BF16).reshape(2, 2, 4, 16, 128)
                    grads[half, y, 2 * k:2 * k + 2, j, 0:4] = tile[:, half]
                tile = products[2][:, y * 128:(y + 1) * 128].astype(BF16).reshape(4, 2, 2, 16, 128)
                grads[half, y, :, j, 4:6] = tile[:, half]
        if l == CHUNKS[i][-1]:
            remote(
                grads.at[1 - at["core"]], bufs[i][1], p_send.at[i, 0], p_recv.at[i, 0], device(peer(at, "core", 1))
            )
            waits.append((bufs[i][1], p_send.at[i, 0]))
            joins.append(i)
        for r0, r1 in ((0, 256), (256, update)):
            taps = contract_columns(gpb[r0:r1], conv[l, 0:C]) + contract_columns(
                later_b[r0:r1], conv[l, C:2 * C]
            )
            gs[r0:r1] = taps + gs[r0:r1]
        for i in ready:
            chunk_join(i)
        for i, _ in INSIDE.get(l, ()):
            stage0(i)
        if l == 3:
            weight_sum()
            weight_send(2, "x", 4)
        if l == 0:
            weight_sum()
            weight_send(3, "z", 7)
    for i in joins:
        chunk_join(i)
    scale = None
    for item in TAIL:
        if item == "scale":
            weight_sum()
            scale = (64.0 * 4.0 * T) / jnp.sum(wtile[4][0:1], axis=1, keepdims=True)
            gs[0:T] = gs[0:T] * scale
            out_copy = pltpu.make_async_copy(gs.at[pl.ds(0, T)], gin_hbm.at[0], out_sem)
            out_copy.start()
        elif item[1] == 0:
            stage0(item[0])
        elif item[1] == 1:
            stage1(item[0])
        elif item[1] == 2:
            stage2(item[0])
        else:
            stage3(item[0], scale)
    out_copy.wait()
    for landing, semaphore in waits:
        wait_all(landing, semaphore)
    for i in range(len(CHUNKS)):
        last_in = bufs[i][10]

        @pl.when(mine)
        def _():
            wait_all(last_in.at[pl.ds(0, 7)], p_send.at[i, 5])

        @pl.when(jnp.logical_not(mine))
        def _():
            wait_all(last_in, p_send.at[i, 5])

    for copy in halo:
        copy.wait_send()
    for group, _, _ in wcopies:
        for copy in group:
            copy.wait_send()


def deliver(gin_ref, parts_ref, gin_out, gconv_out, gout_out):
    gin_out[...] = gin_ref[...]
    core = lax.axis_index("tm") % 2
    gconv_out[...] = parts_ref[:, 0:8]
    gout_out[...] = jnp.where(core == 0, parts_ref[:, 8:12], parts_ref[:, 12:16])


def body(inputs, grad_stream_out, grad_skip_out, sample_weight, conv_weight, out_weight):
    any_spec = pl.BlockSpec(memory_space=pl.ANY)
    vmem_spec = pl.BlockSpec(memory_space=pltpu.VMEM)
    buffers = []
    for chunk in CHUNKS:
        n = len(chunk)
        shapes = (
            (2, 4, 4, n, 6), (4, 4, n, 6), (4, 4, n, 6), (3, 4, n, 3), (3, 4, n, 3), (4, n, 3), (4, n, 3),
            (3, n, 3), (3, n, 3), (4, 2, n), (8, n), (2, 2, 2, n, 3), (2, 2, 2, n, 3),
            (2, 2, n, 3), (2, 2, n, 3), (2, 2, n, 3), (2, 2, n, 3),
        )
        buffers += [pltpu.VMEM(shape + (16, 128), BF16) for shape in shapes]
    gin, parts = pl.pallas_call(
        kernel,
        name="cycle",
        out_shape=(
            jax.ShapeDtypeStruct((1, T, C), F32),
            jax.ShapeDtypeStruct((LAYERS, 16, 128), F32),
        ),
        in_specs=[any_spec] * 6,
        out_specs=(any_spec, vmem_spec),
        scratch_shapes=[
            pltpu.VMEM((EXT, C), BF16),
            pltpu.VMEM((POST, C), BF16),
            pltpu.VMEM((POST, C), BF16),
            pltpu.VMEM((1, T + 128), F32),
            pltpu.VMEM((LAYERS, 2 * C, 2 * C), BF16),
            pltpu.VMEM((LAYERS, C, 2 * C), BF16),
            pltpu.VMEM((32 + HALO + T, C), F32),
            pltpu.VMEM((LAYERS, 32, C), F32),
            pltpu.VMEM((96, C), F32),
            pltpu.VMEM((LAYERS, T, C), BF16),
            pltpu.VMEM((LAYERS, T, C), BF16),
            pltpu.VMEM((LAYERS, POST, C), F32),
            pltpu.VMEM((LAYERS, POST, C), F32),
            pltpu.VMEM((POST, C), F32),
            pltpu.VMEM((POST, 2 * C), BF16),
            pltpu.VMEM((POST + 32, 2 * C), F32),
            pltpu.VMEM((POST, 2 * C), BF16),
            pltpu.VMEM((POST, 2 * C), BF16),
            pltpu.VMEM((5, 8, 128), F32),
            pltpu.VMEM((14, 8, 128), F32),
            pltpu.SemaphoreType.DMA((16,)),
            pltpu.SemaphoreType.DMA((5,)),
            pltpu.SemaphoreType.DMA((5,)),
            pltpu.SemaphoreType.DMA((14,)),
            pltpu.SemaphoreType.DMA((14,)),
            pltpu.SemaphoreType.DMA((len(CHUNKS), 8)),
            pltpu.SemaphoreType.DMA((len(CHUNKS), 8)),
            pltpu.SemaphoreType.DMA,
            *buffers,
        ],
        compiler_params=pltpu.CompilerParams(
            collective_id=0, has_side_effects=True, vmem_limit_bytes=58 << 20
        ),
        cost_estimate=pl.CostEstimate(flops=8 * 10**9, bytes_accessed=8 * 10**6, transcendentals=4 * 10**6),
    )(inputs, grad_stream_out, grad_skip_out, sample_weight, conv_weight, out_weight)
    return pl.pallas_call(
        deliver,
        name="deliver",
        out_shape=(
            jax.ShapeDtypeStruct((1, T, C), F32),
            jax.ShapeDtypeStruct((LAYERS, 8, 128), F32),
            jax.ShapeDtypeStruct((LAYERS, 4, 128), F32),
        ),
        in_specs=[vmem_spec, vmem_spec],
        out_specs=(vmem_spec, vmem_spec, vmem_spec),
    )(gin, parts)


def solution(mesh):
    placed = (
        P("dp", "tm", None),
        P("dp", "tm", None),
        P("dp", "tm", None),
        P("dp", "tm"),
        P(),
        P(),
    )
    return jax.shard_map(
        body,
        mesh=mesh,
        in_specs=placed,
        out_specs=(P("dp", "tm", None), P(None, "tm", "dp"), P(None, "tm", "dp")),
        check_vma=False,
    )
```

time: 51.1 us -> 49.7 us (0.973); the launches traced: 50.4 us -> 49.6 us
  Pallas kernels: 49.8 us -> 48.9 us
    pallas_call x1, Pallas kernels: 47.9 us -> 47.1 us  [body(): pl.pallas_call(kernel, name='cycle', out_shape=(jax.ShapeDtypeStruct((1,...]
where the time goes in v3:
time: 49.7 us; the launch traced here: 49.6 us
  Pallas kernels  48.9 us (98%)
  between operations  0.64 us (1%)
    pallas_call x1, Pallas kernels, body(): pl.pallas_call(kernel, name='cycle', out_shape=(jax.ShapeDtypeStruct((1,...  47.1 us
    pallas_call x1, Pallas kernels, body(): pl.pallas_call(deliver, name='deliver', out_shape=(jax.ShapeDtypeStruct((...  1.88 us

profile of v3, /device:TPU:1, one launch (start us, length us, event | category | flops | bytes accessed | tf_op | source)
XLA Modules:
  0.0 49.6 jit_solution(17261119533824229156)
XLA Ops:
  0.6 47.1 %cycle.1 = (f32[1,512,256]{2,1,0:T(8,128)}, f32[6,16,128]{2,1,0:T(8,128)}) custom-call(bf16[1,512,256]{2,1,0:T(8,128)(2,1)} %x_hbm.1, bf16[1,512,256]{2,1,0:T(8,128)(2,1)} %gso_hbm.1, bf16[1,512,256]{2,1,0:T(8,128)(2,1)} %gsk_hbm.1, f32[1,512]{1,0:T(1,128)} %sw_hbm.1, bf16[6,512,512]{2,1,0:T(8,128)(2,1)} %conv_hbm.1, bf16[6,256,512]{2,1,0:T(8,128)(2,1)} %outw_hbm.1), custom_call_target="tpu_custom_call" | custom-call | flops 8000000000 | bytes 8000000 | tf_op jit(solution)/shard_map/cycle/pallas_call | solution.py:428
  47.7 1.9 %deliver.1 = (f32[1,512,256]{2,1,0:T(8,128)}, f32[6,8,128]{2,1,0:T(8,128)}, f32[6,4,128]{2,1,0:T(4,128)}) custom-call(f32[1,512,256]{2,1,0:T(8,128)} %get-tuple-element.5.gin_ref, f32[6,16,128]{2,1,0:T(8,128)} %get-tuple-element.6.parts_ref), custom_call_target="tpu_custom_call" | custom-call | tf_op jit(solution)/shard_map/deliver/pallas_call | solution.py:473

commit v4 on v3

--- a/solution.py
+++ b/solution.py
@@ -20,10 +20,10 @@
 BUFFERS = 17
 CHUNKS = ((5,), (4, 3), (2, 1), (0,))
 HALVED = (0, 1, 2)
-INSIDE = {1: ((0, 0),)}
+INSIDE = {1: ((0, 0),), 0: ((1, 0), (0, 1))}
 TAIL = (
-    (1, 0), (0, 1), (2, 0), (1, 1), (0, 2), (3, 1), (2, 1), (1, 2), "scale", (0, 3), (3, 2), (2, 2), (1, 3), (3, 3),
-    (2, 3),
+    "x", (2, 0), (1, 1), (0, 2), "z", (3, 1), (2, 1), (1, 2), (3, 2), (2, 2), "scale", (0, 3), (1, 3),
+    (3, 3), (2, 3),
 )
 
 
@@ -69,7 +69,7 @@
     xe, gse, gke, swe, conv, outw,
     stream, tail_s, postb, pres_s, gated_s, filt_s, open_s,
     gs, gproj, gp, gpb, later_b, wtile, wrecv,
-    load_sem, halo_send, halo_recv, w_send, w_recv, p_send, p_recv, out_sem, *rest,
+    load_sem, halo_send, halo_recv, w_send, w_recv, p_send, p_recv, out_sem, known, *rest,
 ):
     bufs = [rest[BUFFERS * i:BUFFERS * (i + 1)] for i in range(len(CHUNKS))]
     at = place()
@@ -80,7 +80,7 @@
     barrier = pltpu.get_barrier_semaphore()
     greet = [nxt, prv, device(peer(at, "core", 1))]
     for axis in "yxz":
-        greet += [device(peer(at, axis, k)) for k in range(1, SIZES[axis])]
+        greet += [device(peer(at, axis, 1)), device(peer(at, axis, SIZES[axis] - 1))]
     for target in greet:
         pl.semaphore_signal(barrier, inc=1, device_id=target, device_id_type=MESH)
 
@@ -97,6 +97,15 @@
         copy.start()
 
     pl.semaphore_wait(barrier, len(greet))
+
+    def tell(step):
+        for k in (1, SIZES["z"] - 1):
+            pl.semaphore_signal(known.at[step], inc=1, device_id=device(peer(at, "z", k)), device_id_type=MESH)
+
+    def hear(step):
+        pl.semaphore_wait(known.at[step], 2)
+
+    tell(0)
     first, final = pl.ds(0, HALO), pl.ds(T, HALO)
     halo = [
         remote(x_hbm.at[0, pl.ds(T - HALO, HALO)], xe.at[first], halo_send.at[0], halo_recv.at[0], nxt),
@@ -197,11 +206,10 @@
             projected = jnp.dot(gated, outw[l, :, 0:C], preferred_element_type=F32)
             stream[32 + lo:32 + hi] += projected[:count]
             postb[32:96] += projected[count:]
-        if l == 1:
-            weight_sum()
-            weight_send(1, "y", 1)
     for i in (2, 3, 4):
         halo[i].wait_recv()
+    hear(0)
+    tell(1)
     weigh(4, HALO)
 
     waits = []
@@ -359,17 +367,18 @@
             gs[r0:r1] = taps + gs[r0:r1]
         for i in ready:
             chunk_join(i)
-        for i, _ in INSIDE.get(l, ()):
-            stage0(i)
-        if l == 3:
+        for i, stage in INSIDE.get(l, ()):
+            (stage0, stage1)[stage](i)
+        if l in (4, 2):
+            hear(3 - l // 2)
+            tell(4 - l // 2)
+        if l == 1:
             weight_sum()
-            weight_send(2, "x", 4)
-        if l == 0:
-            weight_sum()
-            weight_send(3, "z", 7)
+            weight_send(1, "y", 1)
     for i in joins:
         chunk_join(i)
     scale = None
+    hear(3)
     for item in TAIL:
         if item == "scale":
             weight_sum()
@@ -377,6 +386,12 @@
             gs[0:T] = gs[0:T] * scale
             out_copy = pltpu.make_async_copy(gs.at[pl.ds(0, T)], gin_hbm.at[0], out_sem)
             out_copy.start()
+        elif item == "x":
+            weight_sum()
+            weight_send(2, "x", 4)
+        elif item == "z":
+            weight_sum()
+            weight_send(3, "z", 7)
         elif item[1] == 0:
             stage0(item[0])
         elif item[1] == 1:
@@ -463,6 +478,7 @@
             pltpu.SemaphoreType.DMA((len(CHUNKS), 8)),
             pltpu.SemaphoreType.DMA((len(CHUNKS), 8)),
             pltpu.SemaphoreType.DMA,
+            pltpu.SemaphoreType.REGULAR((4,)),
             *buffers,
         ],
         compiler_params=pltpu.CompilerParams(

time: 49.7 us -> 48.2 us (0.970)
  Pallas kernels: 48.9 us -> 47.4 us
    pallas_call x1, Pallas kernels: 47.1 us -> 45.5 us  [body(): pl.pallas_call(kernel, name='cycle', out_shape=(jax.ShapeDtypeStruct((1,...]
where the time goes in v4:
time: 48.2 us; the launch traced here: 48.1 us
  Pallas kernels  47.4 us (98%)
  between operations  0.64 us (1%)
    pallas_call x1, Pallas kernels, body(): pl.pallas_call(kernel, name='cycle', out_shape=(jax.ShapeDtypeStruct((1,...  45.5 us
    pallas_call x1, Pallas kernels, body(): pl.pallas_call(deliver, name='deliver', out_shape=(jax.ShapeDtypeStruct((...  1.88 us

profile of v4, /device:TPU:1, one launch (start us, length us, event | category | flops | bytes accessed | tf_op | source)
XLA Modules:
  0.0 48.1 jit_solution(3217483381659021272)
XLA Ops:
  0.6 45.5 %cycle.1 = (f32[1,512,256]{2,1,0:T(8,128)}, f32[6,16,128]{2,1,0:T(8,128)}) custom-call(bf16[1,512,256]{2,1,0:T(8,128)(2,1)} %x_hbm.1, bf16[1,512,256]{2,1,0:T(8,128)(2,1)} %gso_hbm.1, bf16[1,512,256]{2,1,0:T(8,128)(2,1)} %gsk_hbm.1, f32[1,512]{1,0:T(1,128)} %sw_hbm.1, bf16[6,512,512]{2,1,0:T(8,128)(2,1)} %conv_hbm.1, bf16[6,256,512]{2,1,0:T(8,128)(2,1)} %outw_hbm.1), custom_call_target="tpu_custom_call" | custom-call | flops 8000000000 | bytes 8000000 | tf_op jit(solution)/shard_map/cycle/pallas_call | solution.py:443
  46.2 1.9 %deliver.1 = (f32[1,512,256]{2,1,0:T(8,128)}, f32[6,8,128]{2,1,0:T(8,128)}, f32[6,4,128]{2,1,0:T(4,128)}) custom-call(f32[1,512,256]{2,1,0:T(8,128)} %get-tuple-element.5.gin_ref, f32[6,16,128]{2,1,0:T(8,128)} %get-tuple-element.6.parts_ref), custom_call_target="tpu_custom_call" | custom-call | tf_op jit(solution)/shard_map/deliver/pallas_call | solution.py:489

commit v5 on v4

--- a/solution.py
+++ b/solution.py
@@ -324,6 +324,13 @@
             parts_ref[l] = total[j]
 
     gp[576:608] = jnp.zeros((32, 2 * C), F32)
+    def tap_products(l, update):
+        for r0, r1 in ((0, 256), (256, update)):
+            taps = contract_columns(gpb[r0:r1], conv[l, 0:C]) + contract_columns(
+                later_b[r0:r1], conv[l, C:2 * C]
+            )
+            gs[r0:r1] = taps + gs[r0:r1]
+
     joins = []
     for l in reversed(range(LAYERS)):
         d = 2**l
@@ -360,11 +367,8 @@
             )
             waits.append((bufs[i][1], p_send.at[i, 0]))
             joins.append(i)
-        for r0, r1 in ((0, 256), (256, update)):
-            taps = contract_columns(gpb[r0:r1], conv[l, 0:C]) + contract_columns(
-                later_b[r0:r1], conv[l, C:2 * C]
-            )
-            gs[r0:r1] = taps + gs[r0:r1]
+        if l:
+            tap_products(l, update)
         for i in ready:
             chunk_join(i)
         for i, stage in INSIDE.get(l, ()):
@@ -377,6 +381,7 @@
             weight_send(1, "y", 1)
     for i in joins:
         chunk_join(i)
+    tap_products(0, T)
     scale = None
     hear(3)
     for item in TAIL:

time: 48.2 us -> 48 us (level)
  no operation moved by 1% of the time
where the time goes in v5:
time: 48 us; the launch traced here: 47.9 us
  Pallas kernels  47.2 us (98%)
  between operations  0.64 us (1%)
    pallas_call x1, Pallas kernels, body(): pl.pallas_call(kernel, name='cycle', out_shape=(jax.ShapeDtypeStruct((1,...  45.4 us
    pallas_call x1, Pallas kernels, body(): pl.pallas_call(deliver, name='deliver', out_shape=(jax.ShapeDtypeStruct((...  1.88 us

profile of v5, /device:TPU:1, one launch (start us, length us, event | category | flops | bytes accessed | tf_op | source)
XLA Modules:
  0.0 47.9 jit_solution(16048737879405665467)
XLA Ops:
  0.6 45.4 %cycle.1 = (f32[1,512,256]{2,1,0:T(8,128)}, f32[6,16,128]{2,1,0:T(8,128)}) custom-call(bf16[1,512,256]{2,1,0:T(8,128)(2,1)} %x_hbm.1, bf16[1,512,256]{2,1,0:T(8,128)(2,1)} %gso_hbm.1, bf16[1,512,256]{2,1,0:T(8,128)(2,1)} %gsk_hbm.1, f32[1,512]{1,0:T(1,128)} %sw_hbm.1, bf16[6,512,512]{2,1,0:T(8,128)(2,1)} %conv_hbm.1, bf16[6,256,512]{2,1,0:T(8,128)(2,1)} %outw_hbm.1), custom_call_target="tpu_custom_call" | custom-call | flops 8000000000 | bytes 8000000 | tf_op jit(solution)/shard_map/cycle/pallas_call | solution.py:448
  46.0 1.9 %deliver.1 = (f32[1,512,256]{2,1,0:T(8,128)}, f32[6,8,128]{2,1,0:T(8,128)}, f32[6,4,128]{2,1,0:T(4,128)}) custom-call(f32[1,512,256]{2,1,0:T(8,128)} %get-tuple-element.5.gin_ref, f32[6,16,128]{2,1,0:T(8,128)} %get-tuple-element.6.parts_ref), custom_call_target="tpu_custom_call" | custom-call | tf_op jit(solution)/shard_map/deliver/pallas_call | solution.py:494
